TPU v7x, 256 devices: a whole 4x4x8 slice. The times are simulated.
256 devices in a mesh: sfc: 256 (over y, z, x, core).
Axes of the slice: x: 4, y: 4, z: 8, core: 2. Of those that a mesh axis runs over, the one named last changes fastest.
Arguments:
- fraction: float32 [2048, 4096], P('sfc'), may hold values from 0 to 1
- centroid: float32 [2048, 3, 4096], P('sfc'), may hold values from -0.5 to 0.5
- velocity: float32 [2048, 3, 4096], P('sfc'), may hold values from -4 to 4
- neighbours: int32 [2048, 6], P('sfc'), may hold values from -1 to 2047, as said below
- refinement: int32 [4096, 4], P('sfc'), may hold values from -1 to 2047, as said below
Outputs:
- planes: float32 [2048, 4, 4096], P('sfc')
- reflux: float32 [2048, 6, 2, 256], P('sfc')
Inputs may be any that keep to these rules, and one draw needn't show every extreme that they name: `neighbours`: -1 marks the domain boundary; any other entry is a block on a device at most 2 away along the curve. `refinement`: each row is fine block, direction 0 to 5, coarse block, quadrant 0 to 3. A fine block of -1 marks an empty slot and a device's live slots come first; a live fine block is held by the device that holds the row; the coarse block lies on a device at most 2 away along the curve; every device has a live slot and some device has all 16 live.
All inputs are finite; a program needn't handle non-finite values.
Results may differ from a plain program's by a relative error of at most 0.0003.
Values sent between devices are 32-bit elements; how exact they have to be, the bound alone decides.
No kernel may reach another device: no remote copies, remote signals or barrier semaphores. Data moves between devices by JAX's collectives and lax.ppermute only.
A program may use at most 64 MiB of HBM per device.

v0:
```python
import functools

import jax
import jax.numpy as jnp
from jax import lax
from jax.experimental import pallas as pl
from jax.experimental.pallas import tpu as pltpu
from jax.sharding import PartitionSpec as P

BLK = 8
SLOTS = 16
PASSES = 6
LANES = 128
GROUP = 4
NODES = (0.5 - 3.0**0.5 / 6.0, 0.5 + 3.0**0.5 / 6.0)
TIME_STEP = 0.25
DAMPING = 0.1
VMEM_SPEC = pl.BlockSpec(memory_space=pltpu.VMEM)
SMEM_SPEC = pl.BlockSpec(memory_space=pltpu.SMEM)


def lane_ids():
    return lax.broadcasted_iota(jnp.int32, (8, LANES), 1)


def row_ids():
    return lax.broadcasted_iota(jnp.int32, (8, LANES), 0)


def pick(values, index):
    return jnp.take_along_axis(values, index, axis=1, mode="promise_in_bounds")


def cells(ref, b, xh, yh):
    return ref[pl.ds(xh * 128 + yh * 8 + b, 8, stride=16), :]


def side_index(lane):
    l = lane % 64
    index = jnp.where(l < 16, l, jnp.where(l < 32, l + 96, 16 * (l % 8) + jnp.where(l < 48, 0, 15)))
    upper = ((l >= 16) & (l < 32)) | ((l >= 40) & (l < 48)) | (l >= 56)
    return index, upper


def pack_kernel(frac_ref, cent_ref, refine_ref, out_ref):
    lane = lane_ids()
    index, upper = side_index(lane)

    def block(b, carry):
        for xh in (0, 1):
            sides = []
            for f in range(4):
                ref = frac_ref if f == 0 else cent_ref.at[f - 1]
                half = [cells(ref, b, xh, yh) for yh in (0, 1)]
                for yh in (0, 1):
                    row = half[yh][0:1] if xh == 0 else half[yh][7:8]
                    out_ref[b * 6 + xh, 2 * f + yh : 2 * f + yh + 1, :] = row
                sides.append(jnp.where(upper, pick(half[1], index), pick(half[0], index)))
            for fp in (0, 1):
                out_ref[b * 6 + 2 + 2 * fp + xh] = jnp.where(lane < 64, sides[2 * fp], sides[2 * fp + 1])
        return carry

    lax.fori_loop(0, BLK, block, 0)
    out_ref[48] = jnp.zeros((8, LANES), jnp.float32)
    table = refine_ref[...].astype(jnp.float32)
    out_ref[48, :, 0:4] = table[0:8]
    out_ref[48, :, 4:8] = table[8:16]


def solve(h, g):
    a, b, c = h[0][0], h[0][1], h[1][1]
    ra = 1.0 / (a * c - b * b)
    ia, ib, ic = c * ra, b * ra, a * ra
    p, q, r, s = h[0][2], h[0][3], h[1][2], h[1][3]
    wp, wq = ia * p - ib * r, ia * q - ib * s
    wr, ws = ic * r - ib * p, ic * s - ib * q
    sa = h[2][2] - p * wp - r * wr
    sb = h[2][3] - p * wq - r * ws
    sc = h[3][3] - q * wq - s * ws
    z0, z1 = ia * g[0] - ib * g[1], ic * g[1] - ib * g[0]
    y0 = g[2] - p * z0 - r * z1
    y1 = g[3] - q * z0 - s * z1
    rs = 1.0 / (sa * sc - sb * sb)
    x2 = (sc * y0 - sb * y1) * rs
    x3 = (sa * y1 - sb * y0) * rs
    return z0 - wp * x2 - wq * x3, z1 - wr * x2 - ws * x3, x2, x3


def one_pass(load, params):
    a, b, c, d = params
    h = [[None] * 4 for _ in range(4)]
    g = [None] * 4

    def add(total, value):
        return value if total is None else total + value

    for j in range(7):
        px, py, pz, q = load(j)
        t = jnp.tanh(a * px + b * py + c * pz + d)
        s = 1.0 - t * t
        w = s * s
        r = s * (t + q)
        wx, wy, wz = w * px, w * py, w * pz
        h[0][0] = add(h[0][0], wx * px)
        h[0][1] = add(h[0][1], wx * py)
        h[0][2] = add(h[0][2], wx * pz)
        h[0][3] = add(h[0][3], wx)
        h[1][1] = add(h[1][1], wy * py)
        h[1][2] = add(h[1][2], wy * pz)
        h[1][3] = add(h[1][3], wy)
        h[2][2] = add(h[2][2], wz * pz)
        h[2][3] = add(h[2][3], wz)
        h[3][3] = add(h[3][3], w)
        g[0] = add(g[0], r * px)
        g[1] = add(g[1], r * py)
        g[2] = add(g[2], r * pz)
        g[3] = add(g[3], r)
    for i in range(4):
        h[i][i] = h[i][i] + 4.0 * DAMPING
    step = solve(h, g)
    return tuple(p - u for p, u in zip(params, step))


def start(load):
    f = [0.5 - 0.5 * load(j)[3] for j in range(7)]
    cx, cy, cz, _ = load(0)
    a, b, c = (2.0 * (f[2 * k + 2] - f[2 * k + 1]) for k in range(3))
    d = 2.0 * (2.0 * f[0] - 1.0) - a * cx - b * cy - c * cz
    return a, b, c, d


def stencil(tbl_ref, frac_ref, cent_ref, table, xpad, st):
    lane = lane_ids()
    spread_z = [
        [fh * 64 + jnp.where(lane % 16 == 15, 32, 48) + yh * 8 + lane // 16 for yh in (0, 1)]
        for fh in (0, 1)
    ]
    spread_y = [[fh * 64 + (16 if yh == 0 else 0) + lane % 16 for yh in (0, 1)] for fh in (0, 1)]
    group = (lane % 64) // 16

    def block(b, carry):
        src = [tbl_ref[b * 6 + k] for k in range(6)]
        low, high = table[src[0]], table[src[1]]
        for f in range(4):
            ref = frac_ref if f == 0 else cent_ref.at[f - 1]

            def put(j, xh, yh, value):
                if f == 0:
                    st[j, 3, pl.ds(b * 32 + (xh * 2 + yh) * 8, 8), :] = 1.0 - 2.0 * value
                else:
                    if j > 0 and (j - 1) // 2 == f - 1:
                        value = value + (1.0 if (j - 1) % 2 else -1.0)
                    st[j, f - 1, pl.ds(b * 32 + (xh * 2 + yh) * 8, 8), :] = value

            own = [[cells(ref, b, xh, yh) for yh in (0, 1)] for xh in (0, 1)]
            for yh in (0, 1):
                xpad[f, yh, 7:8, :] = low[2 * f + yh : 2 * f + yh + 1]
                xpad[f, yh, 24:25, :] = high[2 * f + yh : 2 * f + yh + 1]
                for xh in (0, 1):
                    xpad[f, yh, 8 + 8 * xh : 16 + 8 * xh, :] = own[xh][yh]
            for xh in (0, 1):
                ghost = [table[src[k] + 2 * (f // 2) + xh] for k in range(2, 6)]
                mixed = jnp.where(
                    group < 2,
                    jnp.where(group == 0, ghost[1], ghost[0]),
                    jnp.where(group == 2, ghost[3], ghost[2]),
                )
                up = [pltpu.roll(own[xh][yh], 16, 1) for yh in (0, 1)]
                down = [pltpu.roll(own[xh][yh], LANES - 16, 1) for yh in (0, 1)]
                gy = [pick(mixed, spread_y[f % 2][yh]) for yh in (0, 1)]
                for yh in (0, 1):
                    mine = own[xh][yh]
                    gz = pick(mixed, spread_z[f % 2][yh])
                    put(0, xh, yh, mine)
                    put(1, xh, yh, xpad[f, yh, 7 + 8 * xh : 15 + 8 * xh, :])
                    put(2, xh, yh, xpad[f, yh, 9 + 8 * xh : 17 + 8 * xh, :])
                    put(3, xh, yh, jnp.where(lane < 16, gy[0] if yh == 0 else up[0], up[yh]))
                    put(4, xh, yh, jnp.where(lane >= 112, gy[1] if yh == 1 else down[1], down[yh]))
                    put(5, xh, yh, jnp.where(lane % 16 == 0, gz, pltpu.roll(mine, 1, 1)))
                    put(6, xh, yh, jnp.where(lane % 16 == 15, gz, pltpu.roll(mine, LANES - 1, 1)))
        return carry

    lax.fori_loop(0, BLK, block, 0)


def plane_faces(velo_ref, params, pf):
    lane = lane_ids()
    row = row_ids()
    l = lane % 128
    index = jnp.where(
        l < 48, l % 16, jnp.where(l < 64, l + 64, 16 * (l % 8) + jnp.where(l < 80, 0, 15))
    )
    upper = ((l >= 48) & (l < 64)) | ((l >= 72) & (l < 80)) | ((l >= 88) & (l < 96))
    unroll_x = row * 16 + lane % 16

    def block(b, carry):
        def face(first, second, third):
            for h in (0, 1):
                low = pick(jnp.broadcast_to(first[0][h][0:1], (8, LANES)), unroll_x)
                high = pick(jnp.broadcast_to(first[1][h][7:8], (8, LANES)), unroll_x)
                if second is third:
                    zero, one = second[h]
                else:
                    zero = second[h][0], third[h][0]
                    one = second[h][1], third[h][1]
                if second is third:
                    sides = jnp.where(upper, pick(one, index), pick(zero, index))
                else:
                    sides = jnp.where(
                        l < 64,
                        jnp.where(upper, pick(one[0], index), pick(zero[0], index)),
                        jnp.where(upper, pick(one[1], index), pick(zero[1], index)),
                    )
                yield h, jnp.where(l < 16, low, jnp.where(l < 32, high, sides))

        for comp in range(4):
            value = [
                [params[comp, pl.ds(b * 32 + (xh * 2 + yh) * 8, 8), :] for yh in (0, 1)]
                for xh in (0, 1)
            ]
            for h, packed in face(value, value, value):
                pf[b * 5 + comp, 8 * h : 8 * h + 8, :] = packed
        speed = [
            [[cells(velo_ref.at[axis], b, xh, yh) for yh in (0, 1)] for xh in (0, 1)]
            for axis in range(3)
        ]
        for h, packed in face(*speed):
            pf[b * 5 + 4, 8 * h : 8 * h + 8, :] = packed
        return carry

    lax.fori_loop(0, BLK, block, 0)


def fine_slots(refine_ref, pf, slots):
    lane = lane_ids()

    def slot(s, carry):
        f = refine_ref[s * 2]
        k = refine_ref[s * 2 + 1]
        index = k * 16 + 2 * (lane % 8) + (lane // 8) % 2
        odd = (lane // 16) % 2 == 1
        parts = []
        for comp in (lax.shift_right_logical(k, 1), 3, 4):
            even_rows = pf[f * 5 + comp, pl.ds(0, 8, stride=2), :]
            odd_rows = pf[f * 5 + comp, pl.ds(1, 8, stride=2), :]
            parts.append(jnp.where(odd, pick(odd_rows, index), pick(even_rows, index)))
        slots[s] = jnp.where(lane < 32, parts[0], jnp.where(lane < 64, parts[1], parts[2]))
        return carry

    lax.fori_loop(0, SLOTS, slot, 0)


def fit_kernel(
    tbl_ref, refine_ref, own_ref, r1_ref, r2_ref, r3_ref, r4_ref, frac_ref, cent_ref, velo_ref,
    planes_ref, pf_ref, slots_ref, table, xpad, st, params,
):
    lane = lane_ids()
    for at, ref in enumerate((own_ref, r1_ref, r2_ref, r3_ref, r4_ref)):

        def copy(i, carry, at=at, ref=ref):
            for u in range(6):
                table[at * 48 + i * 6 + u] = ref[i * 6 + u]
            return carry

        lax.fori_loop(0, BLK, copy, 0)

    def swap(i, carry):
        for u in range(2, 6):
            v = own_ref[i * 6 + u]
            odd = (lane // 16) % 2 == 1
            table[240 + i * 6 + u] = jnp.where(
                odd, pltpu.roll(v, 16, 1), pltpu.roll(v, LANES - 16, 1)
            )
        return carry

    lax.fori_loop(0, BLK, swap, 0)
    stencil(tbl_ref, frac_ref, cent_ref, table, xpad, st)

    rows = GROUP * 8

    def fit(i, carry):
        at = pl.ds(pl.multiple_of(i * rows, rows), rows)

        def load(j):
            return tuple(st[j, c, at, :] for c in range(4))

        values = lax.fori_loop(0, PASSES, lambda _, p: one_pass(load, p), start(load))
        for comp in range(4):
            params[comp, at, :] = values[comp]
        return carry

    lax.fori_loop(0, 32 // GROUP, fit, 0)

    def emit(b, carry):
        for comp in range(4):
            for xh in (0, 1):
                for yh in (0, 1):
                    planes_ref[pl.ds(b * 128 + 64 * xh + 4 * yh + comp, 8, stride=8), :] = params[
                        comp, pl.ds(b * 32 + (xh * 2 + yh) * 8, 8), :
                    ]
        return carry

    lax.fori_loop(0, BLK, emit, 0)
    plane_faces(velo_ref, params, pf_ref)
    fine_slots(refine_ref, pf_ref, slots_ref)


def moment_kernel(
    meta_ref, pf_ref, s0_ref, s1_ref, s2_ref, s3_ref, s4_ref, out_ref, slots, todo
):
    lane = lane_ids()
    row = row_ids()
    out_ref[...] = jnp.zeros_like(out_ref)
    for at, ref in enumerate((s0_ref, s1_ref, s2_ref, s3_ref, s4_ref)):
        for u in range(SLOTS):
            slots[at * SLOTS + u] = ref[u]
    total = 5 * SLOTS

    def collect(i, n):
        todo[n] = i
        return n + meta_ref[i * 4]

    count = lax.fori_loop(0, total, collect, 0)
    for extra in range(4):
        todo[count + extra] = 0
    quarter = lane // 32
    first_off = (((lane // 16) % 2).astype(jnp.float32) - 0.5) * 0.5
    second_off = (((lane // 8) % 2).astype(jnp.float32) - 0.5) * 0.5

    def group(g, carry):
        fine = [None] * 3
        coarse = [None] * 5
        sign = None
        weight = None
        where = []

        def merge(old, new, q):
            return new if old is None else jnp.where(quarter == q, new, old)

        for q in range(4):
            at = 4 * g + q
            i = todo[at]
            c = meta_ref[i * 4 + 1]
            k = meta_ref[i * 4 + 2]
            quad = meta_ref[i * 4 + 3]
            axis = lax.shift_right_logical(k, 1)
            qa = lax.shift_right_logical(quad, 1)
            qb = quad & 1
            source = slots[i]
            for comp in range(3):
                turn = ((q - comp) * 32) % LANES
                moved = source if turn == 0 else pltpu.roll(source, turn, 1)
                fine[comp] = merge(fine[comp], moved, q)
            index = k * 16 + qb * 8 + lane % 8
            which = (axis, jnp.where(axis == 0, 1, 0), jnp.where(axis == 2, 1, 2), 3, 4)
            for at_comp, comp in enumerate(which):
                value = pf_ref[c * 5 + comp, pl.ds(pl.multiple_of(qa * 8, 8), 8), :]
                coarse[at_comp] = merge(coarse[at_comp], pick(value, index), q)
            s = jnp.where((k & 1) == 1, -1.0, 1.0).astype(jnp.float32)
            sign = merge(sign, jnp.full((8, LANES), s, jnp.float32), q)
            on = jnp.where(at < count, 1.0, 0.0).astype(jnp.float32)
            weight = merge(weight, jnp.full((8, LANES), on, jnp.float32), q)
            where.append((((c * 6 + k) * 2 + qa) * 2, qb))
        an, df, uf = fine
        cn, t1, t2, dc, uc = coarse
        speed = sign * 0.5 * (uf + uc)
        depth = jnp.abs(speed) * TIME_STEP
        outflow = jnp.maximum(speed, 0.0)
        inflow = jnp.minimum(speed, 0.0)
        base = t1 * first_off + t2 * second_off + dc
        volume = 0.0
        moment = 0.0
        for node in NODES:
            fine_phase = an * (sign * (0.5 - node * depth)) + df
            coarse_phase = cn * (-sign * (0.5 - 0.5 * node * depth)) + base
            fine_model = 0.5 * (1.0 + jnp.tanh(fine_phase))
            coarse_model = 0.5 * (1.0 + jnp.tanh(coarse_phase))
            gain = outflow * fine_model
            loss = inflow * coarse_model
            volume = volume + 0.5 * TIME_STEP * (gain + loss)
            moment = moment + 0.5 * TIME_STEP * node * depth * sign * (loss - gain)
        sums = []
        for value in (volume * weight, moment * weight):
            value = value + pltpu.roll(value, LANES - 8, 1)
            sums.append(value + pltpu.roll(value, LANES - 16, 1))
        for q in range(4):
            target, qb = where[q]
            index = 32 * q + lane % 8
            keep = (lane // 16 == row) & ((lane // 8) % 2 == qb)
            rows = [
                jnp.sum(jnp.where(keep, pick(value, index), 0.0), axis=0, keepdims=True)
                for value in sums
            ]
            for m in range(2):
                out_ref[pl.ds(target + m, 1), :] = out_ref[pl.ds(target + m, 1), :] + rows[m]
        return carry

    lax.fori_loop(0, (count + 3) // 4, group, 0)


def partners(n, distance, offset):
    pairs = []
    for i in range(n):
        up = ((i - offset) // distance) % 2 == 0
        pairs.append((i, (i + distance if up else i - distance) % n))
    return pairs


def trade(value):
    n = lax.axis_size("sfc")
    return [
        lax.ppermute(value, "sfc", partners(n, distance, offset))
        for distance, offset in ((1, 0), (1, 1), (2, 0), (2, 2))
    ]


def tiles(field):
    return field.reshape(BLK, 32, LANES).transpose(1, 0, 2).reshape(256, LANES)


def tiles3(field):
    return field.reshape(BLK, 3, 32, LANES).transpose(1, 2, 0, 3).reshape(3, 256, LANES)


def per_device(fraction, centroid, velocity, neighbours, refinement):
    f32 = jnp.float32
    i32 = jnp.int32
    me = lax.axis_index("sfc").astype(i32)
    frac, cent, velo = tiles(fraction), tiles3(centroid), tiles3(velocity)
    out = functools.partial(jax.ShapeDtypeStruct, dtype=f32)
    limit = pltpu.CompilerParams(vmem_limit_bytes=48 << 20)

    faces = pl.pallas_call(
        pack_kernel,
        out_shape=out((49, 8, LANES)),
        in_specs=[VMEM_SPEC] * 3,
        out_specs=VMEM_SPEC,
        compiler_params=limit,
        name="pack",
    )(frac, cent, refinement)
    got = trade(faces)

    offset = neighbours // BLK - me
    odd = me % 2
    odd2 = (me // 2) % 2
    near = jnp.where(offset == 1 - 2 * odd, 1, 2)
    far = jnp.where(offset == 2 - 4 * odd2, 3, 4)
    part = jnp.where(offset == 0, 0, jnp.where(jnp.abs(offset) == 1, near, far))
    direction = jnp.arange(6, dtype=i32)[None, :]
    block = jnp.arange(BLK, dtype=i32)[:, None]
    inside = part * BLK + neighbours % BLK
    x_row = jnp.where(neighbours >= 0, inside * 6 + 1 - direction, block * 6 + direction)
    yz_row = jnp.where(neighbours >= 0, inside, 40 + block) * 6 + 2
    rows = jnp.where(direction < 2, x_row, yz_row)
    rows = jnp.clip(rows, 0, 285).reshape(48)

    fine_local = jnp.clip(refinement[:, 0] - me * BLK, 0, BLK - 1)
    fine_side = jnp.clip(refinement[:, 1], 0, 5)
    fine_table = jnp.stack([fine_local, fine_side], axis=1).reshape(2 * SLOTS)

    planes, plane_face, slots = pl.pallas_call(
        fit_kernel,
        out_shape=(out((1024, LANES)), out((BLK * 5, 16, LANES)), out((SLOTS, 8, LANES))),
        in_specs=[SMEM_SPEC] * 2 + [VMEM_SPEC] * 8,
        out_specs=(VMEM_SPEC,) * 3,
        scratch_shapes=[
            pltpu.VMEM((288, 8, LANES), f32),
            pltpu.VMEM((4, 2, 32, LANES), f32),
            pltpu.VMEM((7, 4, 256, LANES), f32),
            pltpu.VMEM((4, 256, LANES), f32),
        ],
        compiler_params=limit,
        name="fit",
    )(rows, fine_table, faces, *got, frac, cent, velo)

    got_slots = trade(slots)
    tables = [refinement] + [
        jnp.concatenate([v[48, :, 0:4], v[48, :, 4:8]], axis=0).astype(i32) for v in got
    ]
    table = jnp.concatenate(tables, axis=0)
    mine = (table[:, 0] >= 0) & (table[:, 2] // BLK == me)
    side = jnp.clip(table[:, 1], 0, 5)
    meta = jnp.stack(
        [
            mine.astype(i32),
            jnp.clip(table[:, 2], 0, None) % BLK,
            side + 1 - 2 * (side % 2),
            jnp.clip(table[:, 3], 0, 3),
        ],
        axis=1,
    ).reshape(4 * 5 * SLOTS)

    reflux = pl.pallas_call(
        moment_kernel,
        out_shape=out((BLK * 6 * 4, LANES)),
        in_specs=[SMEM_SPEC] + [VMEM_SPEC] * 6,
        out_specs=VMEM_SPEC,
        scratch_shapes=[
            pltpu.VMEM((5 * SLOTS, 8, LANES), f32),
            pltpu.SMEM((5 * SLOTS + 8,), i32),
        ],
        compiler_params=limit,
        name="moments",
    )(meta, plane_face, slots, *got_slots)

    planes = planes.reshape(BLK, 32, 4, LANES).transpose(0, 2, 1, 3).reshape(BLK, 4, 4096)
    reflux = reflux.reshape(BLK, 6, 2, 2, LANES).transpose(0, 1, 3, 2, 4).reshape(BLK, 6, 2, 256)
    return planes, reflux


def solution(mesh):
    return jax.shard_map(
        per_device,
        mesh=mesh,
        in_specs=(
            P("sfc", None),
            P("sfc", None, None),
            P("sfc", None, None),
            P("sfc", None),
            P("sfc", None),
        ),
        out_specs=(P("sfc", None, None), P("sfc", None, None, None)),
        check_vma=False,
    )
```

profile of v0, /device:TPU:0, one launch (start us, length us, event | category | flops | bytes accessed | tf_op | source)
XLA Modules:
  0.0 57.7 jit_solution(2093425472455779031)
XLA Ops:
  0.6 0.8 %copy.20.refine_ref = s32[16,4]{1,0:T(8,128)S(1)} copy(s32[16,4]{0,1:T(4,128)} %param.9) | data formatting | bytes 512 | tf_op args[4]
  1.4 1.0 %copy-done = f32[8,3,4096]{2,0,1:T(8,128)S(1)} copy-done((f32[8,3,4096]{2,0,1:T(8,128)S(1)}, f32[8,3,4096]{2,0,1:T(8,128)}, u32[]{:S(2)}) %copy-start) | copy-done | bytes 393240
  2.4 0.9 %copy-done.2 = f32[8,4096]{1,0:T(8,128)S(1)} copy-done((f32[8,4096]{1,0:T(8,128)S(1)}, f32[8,4096]{1,0:T(8,128)}, u32[]{:S(2)}) %copy-start.2) | copy-done | bytes 131096
  3.3 0.7 %pack.1.own_ref = f32[49,8,128]{2,1,0:T(8,128)S(1)} custom-call(f32[256,128]{1,0:T(8,128)S(1)} %bitcast.35, f32[3,256,128]{2,1,0:T(8,128)S(1)} %bitcast.33, s32[16,4]{1,0:T(8,128)S(1)} %copy.20.refine_ref), custom_call_target="tpu_custom_call" | custom-call | tf_op jit(solution)/shard_map/pack/pallas_call | solution.py:433
  4.0 0.1 collective-permute-start
  4.1 8.9 %collective-permute-start.1 = (f32[49,8,128]{2,1,0:T(8,128)S(1)}, f32[49,8,128]{2,1,0:T(8,128)S(1)}, u32[]{:S(2)}, u32[]{:S(2)}) collective-permute-start(f32[49,8,128]{2,1,0:T(8,128)S(1)} %pack.1.own_ref), channel_id=1, source_target_pairs={{0,255},{1,2},{2,1},{3,4},{4,3},{5,6},{6,5},{7,8},{8,7},{9,10},{10... | collective-permute-start | bytes 602120 | tf_op jit(solution)/shard_map/ppermute | solution.py:412
  13.0 1.4 %collective-permute-start.3 = (f32[49,8,128]{2,1,0:T(8,128)S(1)}, f32[49,8,128]{2,1,0:T(8,128)S(1)}, u32[]{:S(2)}, u32[]{:S(2)}) collective-permute-start(f32[49,8,128]{2,1,0:T(8,128)S(1)} %pack.1.own_ref), channel_id=1, source_target_pairs={{0,254},{1,255},{2,4},{3,5},{4,2},{5,3},{6,8},{7,9},{8,6},{9,7},{1... | collective-permute-start | bytes 602120 | tf_op jit(solution)/shard_map/ppermute | solution.py:412
  14.4 0.7 %copy-done.6 = s32[8,6]{1,0:T(8,128)S(1)} copy-done((s32[8,6]{1,0:T(8,128)S(1)}, s32[8,6]{1,0:T(8,128)}, u32[]{:S(2)}) %copy-start.6) | copy-done | bytes 216
  15.2 0.1 reshape.58.tbl_ref
  15.3 0.1 copy.19
  15.3 0.1 reshape.59.refine_ref
  15.5 0.1 copy.23
  15.6 0.1 copy.22
  15.7 1.9 %collective-permute-done.1.r2_ref = f32[49,8,128]{2,1,0:T(8,128)S(1)} collective-permute-done((f32[49,8,128]{2,1,0:T(8,128)S(1)}, f32[49,8,128]{2,1,0:T(8,128)S(1)}, u32[]{:S(2)}, u32[]{:S(2)}) %collective-permute-start.1) | collective-permute-done | bytes 200736 | tf_op jit(solution)/shard_map/ppermute | solution.py:412
  17.6 0.1 copy.25
  17.7 0.1 copy.24
  17.8 0.9 %collective-permute-done.2.r3_ref = f32[49,8,128]{2,1,0:T(8,128)S(1)} collective-permute-done((f32[49,8,128]{2,1,0:T(8,128)S(1)}, f32[49,8,128]{2,1,0:T(8,128)S(1)}, u32[]{:S(2)}, u32[]{:S(2)}) %collective-permute-start.2) | collective-permute-done | bytes 200736 | tf_op jit(solution)/shard_map/ppermute | solution.py:412
  18.8 0.1 copy.27
  18.9 0.1 copy.26
  19.0 5.2 %collective-permute-done.3.r4_ref = f32[49,8,128]{2,1,0:T(8,128)S(1)} collective-permute-done((f32[49,8,128]{2,1,0:T(8,128)S(1)}, f32[49,8,128]{2,1,0:T(8,128)S(1)}, u32[]{:S(2)}, u32[]{:S(2)}) %collective-permute-start.3) | collective-permute-done | bytes 200736 | tf_op jit(solution)/shard_map/ppermute | solution.py:412
  24.2 0.1 copy.29
  24.3 0.1 copy.28
  24.4 0.1 maximum_convert_fusion
  24.5 0.1 maximum_convert_fusion.2
  24.5 0.1 concatenate.19
  24.7 16.7 %fit.1 = (f32[1024,128]{1,0:T(8,128)}, f32[40,16,128]{2,1,0:T(8,128)S(1)}, f32[16,8,128]{2,1,0:T(8,128)S(1)}) custom-call(s32[48]{0:T(128)S(1)} %reshape.58.tbl_ref, s32[32]{0:T(128)S(1)} %reshape.59.refine_ref, f32[49,8,128]{2,1,0:T(8,128)S(1)} %pack.1.own_ref, f32[49,8,128]{2,1,0:T(8,128)S(1)} %collective-permute-done.r1_ref, ...), custom_call_target="tpu_custom_call" | custom-call | tf_op jit(solution)/shard_map/fit/pallas_call | solution.py:461
  41.4 4.4 %collective-permute-start.5 = (f32[16,8,128]{2,1,0:T(8,128)S(1)}, f32[16,8,128]{2,1,0:T(8,128)S(1)}, u32[]{:S(2)}, u32[]{:S(2)}) collective-permute-start(f32[16,8,128]{2,1,0:T(8,128)S(1)} %get-tuple-element.7.s0_ref), channel_id=1, source_target_pairs={{0,255},{1,2},{2,1},{3,4},{4,3},{5,6},{6,5},{7,8},{8,7},{9,10},{10... | collective-permute-start | bytes 196616 | tf_op jit(solution)/shard_map/ppermute | solution.py:412
  45.9 0.1 copy.30
  46.0 0.1 reshape.68.meta_ref
  46.1 4.5 %collective-permute-done.5.s2_ref = f32[16,8,128]{2,1,0:T(8,128)S(1)} collective-permute-done((f32[16,8,128]{2,1,0:T(8,128)S(1)}, f32[16,8,128]{2,1,0:T(8,128)S(1)}, u32[]{:S(2)}, u32[]{:S(2)}) %collective-permute-start.5) | collective-permute-done | bytes 65568 | tf_op jit(solution)/shard_map/ppermute | solution.py:412
  50.5 5.0 %collective-permute-done.7.s4_ref = f32[16,8,128]{2,1,0:T(8,128)S(1)} collective-permute-done((f32[16,8,128]{2,1,0:T(8,128)S(1)}, f32[16,8,128]{2,1,0:T(8,128)S(1)}, u32[]{:S(2)}, u32[]{:S(2)}) %collective-permute-start.7) | collective-permute-done | bytes 65568 | tf_op jit(solution)/shard_map/ppermute | solution.py:412
  55.5 2.1 %moments.1 = f32[192,128]{1,0:T(8,128)} custom-call(s32[320]{0:T(512)S(1)} %reshape.68.meta_ref, f32[40,16,128]{2,1,0:T(8,128)S(1)} %get-tuple-element.6.pf_ref, f32[16,8,128]{2,1,0:T(8,128)S(1)} %get-tuple-element.7.s0_ref, f32[16,8,128]{2,1,0:T(8,128)S(1)} %collective-permute-done.4.s1_ref, f32[16,8,128]{2,1,0:T(8,128)S(1)} %collective-permute-done.5.s2_ref, ...), custom_call_target="tpu_custom_call" | custom-call | tf_op jit(solution)/shard_map/moments/pallas_call | solution.py:493
  (30 shorter events, 0.5 us)
Async XLA Ops:
  1.4 1.0 %copy-start = (f32[8,3,4096]{2,0,1:T(8,128)S(1)}, f32[8,3,4096]{2,0,1:T(8,128)}, u32[]{:S(2)}) copy-start(f32[8,3,4096]{2,0,1:T(8,128)} %param.6) | copy-start | bytes 1179652
  2.4 0.9 %copy-start.2 = (f32[8,4096]{1,0:T(8,128)S(1)}, f32[8,4096]{1,0:T(8,128)}, u32[]{:S(2)}) copy-start(f32[8,4096]{1,0:T(8,128)} %param.5) | copy-start | bytes 393220
  3.3 21.4 %copy-start.1 = (f32[8,3,4096]{2,0,1:T(8,128)S(1)}, f32[8,3,4096]{2,0,1:T(8,128)}, u32[]{:S(2)}) copy-start(f32[8,3,4096]{2,0,1:T(8,128)} %param.6) | copy-start | bytes 1179652
  3.3 21.4 %copy-start.4 = (f32[8,3,4096]{2,0,1:T(8,128)S(1)}, f32[8,3,4096]{2,0,1:T(8,128)}, u32[]{:S(2)}) copy-start(f32[8,3,4096]{2,0,1:T(8,128)} %param.7) | copy-start | bytes 1179652
  4.0 11.4 %collective-permute-start = (f32[49,8,128]{2,1,0:T(8,128)S(1)}, f32[49,8,128]{2,1,0:T(8,128)S(1)}, u32[]{:S(2)}, u32[]{:S(2)}) collective-permute-start(f32[49,8,128]{2,1,0:T(8,128)S(1)} %pack.1.own_ref), channel_id=1, source_target_pairs={{0,1},{1,0},{2,3},{3,2},{4,5},{5,4},{6,7},{7,6},{8,9},{9,8},{10,11... | collective-permute-start | bytes 602120 | tf_op jit(solution)/shard_map/ppermute | solution.py:412
  4.1 13.4 %collective-permute-start.1 = (f32[49,8,128]{2,1,0:T(8,128)S(1)}, f32[49,8,128]{2,1,0:T(8,128)S(1)}, u32[]{:S(2)}, u32[]{:S(2)}) collective-permute-start(f32[49,8,128]{2,1,0:T(8,128)S(1)} %pack.1.own_ref), channel_id=1, source_target_pairs={{0,255},{1,2},{2,1},{3,4},{4,3},{5,6},{6,5},{7,8},{8,7},{9,10},{10... | collective-permute-start | bytes 602120 | tf_op jit(solution)/shard_map/ppermute | solution.py:412
  13.0 5.7 %collective-permute-start.2 = (f32[49,8,128]{2,1,0:T(8,128)S(1)}, f32[49,8,128]{2,1,0:T(8,128)S(1)}, u32[]{:S(2)}, u32[]{:S(2)}) collective-permute-start(f32[49,8,128]{2,1,0:T(8,128)S(1)} %pack.1.own_ref), channel_id=1, source_target_pairs={{0,2},{1,3},{2,0},{3,1},{4,6},{5,7},{6,4},{7,5},{8,10},{9,11},{10,... | collective-permute-start | bytes 602120 | tf_op jit(solution)/shard_map/ppermute | solution.py:412
  13.0 11.1 %collective-permute-start.3 = (f32[49,8,128]{2,1,0:T(8,128)S(1)}, f32[49,8,128]{2,1,0:T(8,128)S(1)}, u32[]{:S(2)}, u32[]{:S(2)}) collective-permute-start(f32[49,8,128]{2,1,0:T(8,128)S(1)} %pack.1.own_ref), channel_id=1, source_target_pairs={{0,254},{1,255},{2,4},{3,5},{4,2},{5,3},{6,8},{7,9},{8,6},{9,7},{1... | collective-permute-start | bytes 602120 | tf_op jit(solution)/shard_map/ppermute | solution.py:412
  14.4 0.8 %copy-start.5 = (s32[16,4]{0,1:T(4,128)S(1)}, s32[16,4]{0,1:T(4,128)}, u32[]{:S(2)}) copy-start(s32[16,4]{0,1:T(4,128)} %param.9) | copy-start | bytes 772
  14.4 0.7 %copy-start.6 = (s32[8,6]{1,0:T(8,128)S(1)}, s32[8,6]{1,0:T(8,128)}, u32[]{:S(2)}) copy-start(s32[8,6]{1,0:T(8,128)} %param.8) | copy-start | bytes 580
  14.4 10.3 %copy-start.3 = (f32[8,4096]{1,0:T(8,128)S(1)}, f32[8,4096]{1,0:T(8,128)}, u32[]{:S(2)}) copy-start(f32[8,4096]{1,0:T(8,128)} %param.5) | copy-start | bytes 393220
  41.4 4.7 %collective-permute-start.4 = (f32[16,8,128]{2,1,0:T(8,128)S(1)}, f32[16,8,128]{2,1,0:T(8,128)S(1)}, u32[]{:S(2)}, u32[]{:S(2)}) collective-permute-start(f32[16,8,128]{2,1,0:T(8,128)S(1)} %get-tuple-element.7.s0_ref), channel_id=1, source_target_pairs={{0,1},{1,0},{2,3},{3,2},{4,5},{5,4},{6,7},{7,6},{8,9},{9,8},{10,11... | collective-permute-start | bytes 196616 | tf_op jit(solution)/shard_map/ppermute | solution.py:412
  41.4 9.1 %collective-permute-start.5 = (f32[16,8,128]{2,1,0:T(8,128)S(1)}, f32[16,8,128]{2,1,0:T(8,128)S(1)}, u32[]{:S(2)}, u32[]{:S(2)}) collective-permute-start(f32[16,8,128]{2,1,0:T(8,128)S(1)} %get-tuple-element.7.s0_ref), channel_id=1, source_target_pairs={{0,255},{1,2},{2,1},{3,4},{4,3},{5,6},{6,5},{7,8},{8,7},{9,10},{10... | collective-permute-start | bytes 196616 | tf_op jit(solution)/shard_map/ppermute | solution.py:412
  45.8 4.7 %collective-permute-start.6 = (f32[16,8,128]{2,1,0:T(8,128)S(1)}, f32[16,8,128]{2,1,0:T(8,128)S(1)}, u32[]{:S(2)}, u32[]{:S(2)}) collective-permute-start(f32[16,8,128]{2,1,0:T(8,128)S(1)} %get-tuple-element.7.s0_ref), channel_id=1, source_target_pairs={{0,2},{1,3},{2,0},{3,1},{4,6},{5,7},{6,4},{7,5},{8,10},{9,11},{10,... | collective-permute-start | bytes 196616 | tf_op jit(solution)/shard_map/ppermute | solution.py:412
  45.8 9.7 %collective-permute-start.7 = (f32[16,8,128]{2,1,0:T(8,128)S(1)}, f32[16,8,128]{2,1,0:T(8,128)S(1)}, u32[]{:S(2)}, u32[]{:S(2)}) collective-permute-start(f32[16,8,128]{2,1,0:T(8,128)S(1)} %get-tuple-element.7.s0_ref), channel_id=1, source_target_pairs={{0,254},{1,255},{2,4},{3,5},{4,2},{5,3},{6,8},{7,9},{8,6},{9,7},{1... | collective-permute-start | bytes 196616 | tf_op jit(solution)/shard_map/ppermute | solution.py:412
where the time goes:
time: 58.2 us; the launch traced here: 57.7 us
  Pallas kernels  19.6 us (34%)
  waiting for transfers between devices  17.5 us (30%)
  starting transfers between devices  14.8 us (25%)
  local copies, waits for them, and re-layouts  4.84 us (8%)
  between operations  0.75 us (1%)
    ppermute x8, waiting for transfers between devices, trade(): lax.ppermute(value, 'sfc', partners(n, distance, offset))  17.5 us
    pallas_call x1, Pallas kernels, per_device(): pl.pallas_call(fit_kernel, out_shape=(out((1024, LANES)), out((BLK * 5, 1...  16.7 us
    ppermute x8, starting transfers between devices, trade(): lax.ppermute(value, 'sfc', partners(n, distance, offset))  14.8 us
    unnamed x15, local copies, waits for them, and re-layouts  3.34 us
    pallas_call x1, Pallas kernels, per_device(): pl.pallas_call(moment_kernel, out_shape=out((BLK * 6 * 4, LANES)), in_spe...  2.14 us
  transfers between devices with their start and end apart: 8, of which 5 were waited for; matrix products, arithmetic and copies ran while one was open for 2% of the time, Pallas kernels for 0%

commit v1 on v0

--- a/solution.py
+++ b/solution.py
@@ -9,6 +9,7 @@
 
 BLK = 8
 SLOTS = 16
+PARTS = 6
 PASSES = 6
 LANES = 128
 GROUP = 4
@@ -42,16 +43,26 @@
     return index, upper
 
 
-def pack_kernel(frac_ref, cent_ref, refine_ref, out_ref):
+def pack_kernel(frac_hbm, cent_hbm, refine_hbm, out_ref, field, refine_ref, sems):
+    copies = [
+        pltpu.make_async_copy(frac_hbm if f == 0 else cent_hbm.at[f - 1], field.at[f], sems.at[f])
+        for f in range(4)
+    ]
+    copies.append(pltpu.make_async_copy(refine_hbm, refine_ref, sems.at[4]))
+    for copy in copies:
+        copy.start()
     lane = lane_ids()
     index, upper = side_index(lane)
+    out_ref[48] = jnp.zeros((8, LANES), jnp.float32)
+    for copy in copies:
+        copy.wait()
+    out_ref[48, 0:4, 0:SLOTS] = refine_ref[...].astype(jnp.float32)
 
     def block(b, carry):
         for xh in (0, 1):
             sides = []
             for f in range(4):
-                ref = frac_ref if f == 0 else cent_ref.at[f - 1]
-                half = [cells(ref, b, xh, yh) for yh in (0, 1)]
+                half = [cells(field.at[f], b, xh, yh) for yh in (0, 1)]
                 for yh in (0, 1):
                     row = half[yh][0:1] if xh == 0 else half[yh][7:8]
                     out_ref[b * 6 + xh, 2 * f + yh : 2 * f + yh + 1, :] = row
@@ -61,10 +72,6 @@
         return carry
 
     lax.fori_loop(0, BLK, block, 0)
-    out_ref[48] = jnp.zeros((8, LANES), jnp.float32)
-    table = refine_ref[...].astype(jnp.float32)
-    out_ref[48, :, 0:4] = table[0:8]
-    out_ref[48, :, 4:8] = table[8:16]
 
 
 def solve(h, g):
@@ -247,15 +254,15 @@
         slots[s] = jnp.where(lane < 32, parts[0], jnp.where(lane < 64, parts[1], parts[2]))
         return carry
 
-    lax.fori_loop(0, SLOTS, slot, 0)
+    lax.fori_loop(0, SLOTS, slot, 0, unroll=4)
 
 
 def fit_kernel(
-    tbl_ref, refine_ref, own_ref, r1_ref, r2_ref, r3_ref, r4_ref, frac_ref, cent_ref, velo_ref,
+    tbl_ref, refine_ref, own_ref, r1_ref, r2_ref, r3_ref, r4_ref, r5_ref, frac_ref, cent_ref, velo_ref,
     planes_ref, pf_ref, slots_ref, table, xpad, st, params,
 ):
     lane = lane_ids()
-    for at, ref in enumerate((own_ref, r1_ref, r2_ref, r3_ref, r4_ref)):
+    for at, ref in enumerate((own_ref, r1_ref, r2_ref, r3_ref, r4_ref, r5_ref)):
 
         def copy(i, carry, at=at, ref=ref):
             for u in range(6):
@@ -268,7 +275,7 @@
         for u in range(2, 6):
             v = own_ref[i * 6 + u]
             odd = (lane // 16) % 2 == 1
-            table[240 + i * 6 + u] = jnp.where(
+            table[288 + i * 6 + u] = jnp.where(
                 odd, pltpu.roll(v, 16, 1), pltpu.roll(v, LANES - 16, 1)
             )
         return carry
@@ -306,21 +313,21 @@
 
 
 def moment_kernel(
-    meta_ref, pf_ref, s0_ref, s1_ref, s2_ref, s3_ref, s4_ref, out_ref, slots, todo
+    meta_ref, pf_ref, s0_ref, s1_ref, s2_ref, s3_ref, s4_ref, s5_ref, out_ref, slots, todo
 ):
     lane = lane_ids()
     row = row_ids()
     out_ref[...] = jnp.zeros_like(out_ref)
-    for at, ref in enumerate((s0_ref, s1_ref, s2_ref, s3_ref, s4_ref)):
+    for at, ref in enumerate((s0_ref, s1_ref, s2_ref, s3_ref, s4_ref, s5_ref)):
         for u in range(SLOTS):
             slots[at * SLOTS + u] = ref[u]
-    total = 5 * SLOTS
+    total = PARTS * SLOTS
 
     def collect(i, n):
         todo[n] = i
-        return n + meta_ref[i * 4]
-
-    count = lax.fori_loop(0, total, collect, 0)
+        return n + meta_ref[i]
+
+    count = lax.fori_loop(0, total, collect, 0, unroll=8)
     for extra in range(4):
         todo[count + extra] = 0
     quarter = lane // 32
@@ -340,9 +347,9 @@
         for q in range(4):
             at = 4 * g + q
             i = todo[at]
-            c = meta_ref[i * 4 + 1]
-            k = meta_ref[i * 4 + 2]
-            quad = meta_ref[i * 4 + 3]
+            c = meta_ref[total + i]
+            k = meta_ref[2 * total + i]
+            quad = meta_ref[3 * total + i]
             axis = lax.shift_right_logical(k, 1)
             qa = lax.shift_right_logical(quad, 1)
             qb = quad & 1
@@ -402,16 +409,20 @@
     pairs = []
     for i in range(n):
         up = ((i - offset) // distance) % 2 == 0
-        pairs.append((i, (i + distance if up else i - distance) % n))
+        j = i + distance if up else i - distance
+        pairs.append((i, j if 0 <= j < n else i ^ 1))
     return pairs
 
 
 def trade(value):
     n = lax.axis_size("sfc")
-    return [
-        lax.ppermute(value, "sfc", partners(n, distance, offset))
-        for distance, offset in ((1, 0), (1, 1), (2, 0), (2, 2))
-    ]
+    inside, near, far = partners(n, 1, 0), partners(n, 2, 0), partners(n, 2, 2)
+    far_same = lax.ppermute(value, "sfc", far)
+    near_same = lax.ppermute(value, "sfc", near)
+    sibling = lax.ppermute(value, "sfc", inside)
+    far_other = lax.ppermute(far_same, "sfc", inside)
+    near_other = lax.ppermute(near_same, "sfc", inside)
+    return [sibling, near_same, far_same, near_other, far_other]
 
 
 def tiles(field):
@@ -433,26 +444,33 @@
     faces = pl.pallas_call(
         pack_kernel,
         out_shape=out((49, 8, LANES)),
-        in_specs=[VMEM_SPEC] * 3,
+        in_specs=[pl.BlockSpec(memory_space=pltpu.HBM)] * 3,
         out_specs=VMEM_SPEC,
+        scratch_shapes=[
+            pltpu.VMEM((4, 256, LANES), f32),
+            pltpu.VMEM((4, SLOTS), i32),
+            pltpu.SemaphoreType.DMA((5,)),
+        ],
         compiler_params=limit,
         name="pack",
-    )(frac, cent, refinement)
+    )(*(pltpu.with_memory_space_constraint(v, pltpu.HBM) for v in (frac, cent, refinement.T)))
     got = trade(faces)
 
-    offset = neighbours // BLK - me
-    odd = me % 2
-    odd2 = (me // 2) % 2
-    near = jnp.where(offset == 1 - 2 * odd, 1, 2)
-    far = jnp.where(offset == 2 - 4 * odd2, 3, 4)
-    part = jnp.where(offset == 0, 0, jnp.where(jnp.abs(offset) == 1, near, far))
+    device = neighbours // BLK
+    step = device // 2 - me // 2
+    near_step = 1 - 2 * ((me // 2) % 2)
+    part = jnp.where(
+        step == 0,
+        jnp.where(device == me, 0, 1),
+        jnp.where(step == near_step, 2, 3) + jnp.where(device % 2 == me % 2, 0, 2),
+    )
     direction = jnp.arange(6, dtype=i32)[None, :]
     block = jnp.arange(BLK, dtype=i32)[:, None]
     inside = part * BLK + neighbours % BLK
     x_row = jnp.where(neighbours >= 0, inside * 6 + 1 - direction, block * 6 + direction)
-    yz_row = jnp.where(neighbours >= 0, inside, 40 + block) * 6 + 2
+    yz_row = jnp.where(neighbours >= 0, inside, 48 + block) * 6 + 2
     rows = jnp.where(direction < 2, x_row, yz_row)
-    rows = jnp.clip(rows, 0, 285).reshape(48)
+    rows = jnp.clip(rows, 0, 333).reshape(48)
 
     fine_local = jnp.clip(refinement[:, 0] - me * BLK, 0, BLK - 1)
     fine_side = jnp.clip(refinement[:, 1], 0, 5)
@@ -461,10 +479,10 @@
     planes, plane_face, slots = pl.pallas_call(
         fit_kernel,
         out_shape=(out((1024, LANES)), out((BLK * 5, 16, LANES)), out((SLOTS, 8, LANES))),
-        in_specs=[SMEM_SPEC] * 2 + [VMEM_SPEC] * 8,
+        in_specs=[SMEM_SPEC] * 2 + [VMEM_SPEC] * 9,
         out_specs=(VMEM_SPEC,) * 3,
         scratch_shapes=[
-            pltpu.VMEM((288, 8, LANES), f32),
+            pltpu.VMEM((336, 8, LANES), f32),
             pltpu.VMEM((4, 2, 32, LANES), f32),
             pltpu.VMEM((7, 4, 256, LANES), f32),
             pltpu.VMEM((4, 256, LANES), f32),
@@ -474,30 +492,32 @@
     )(rows, fine_table, faces, *got, frac, cent, velo)
 
     got_slots = trade(slots)
-    tables = [refinement] + [
-        jnp.concatenate([v[48, :, 0:4], v[48, :, 4:8]], axis=0).astype(i32) for v in got
-    ]
-    table = jnp.concatenate(tables, axis=0)
-    mine = (table[:, 0] >= 0) & (table[:, 2] // BLK == me)
-    side = jnp.clip(table[:, 1], 0, 5)
+    count = lax.axis_size("sfc")
+    twice = (me // 2 == 0) | (me // 2 == count // 2 - 1)
+    tables = jnp.stack(
+        [refinement.T] + [v[48, 0:4, 0:SLOTS].astype(i32) for v in got], axis=1
+    )
+    part_ids = jnp.arange(PARTS, dtype=i32)[:, None]
+    fresh = jnp.logical_not(twice & ((part_ids == 3) | (part_ids == 5)))
+    mine = (tables[0] >= 0) & (tables[2] // BLK == me) & fresh
+    side = jnp.clip(tables[1], 0, 5)
     meta = jnp.stack(
         [
             mine.astype(i32),
-            jnp.clip(table[:, 2], 0, None) % BLK,
+            jnp.clip(tables[2], 0, None) % BLK,
             side + 1 - 2 * (side % 2),
-            jnp.clip(table[:, 3], 0, 3),
-        ],
-        axis=1,
-    ).reshape(4 * 5 * SLOTS)
+            jnp.clip(tables[3], 0, 3),
+        ]
+    ).reshape(4 * PARTS * SLOTS)
 
     reflux = pl.pallas_call(
         moment_kernel,
         out_shape=out((BLK * 6 * 4, LANES)),
-        in_specs=[SMEM_SPEC] + [VMEM_SPEC] * 6,
+        in_specs=[SMEM_SPEC] + [VMEM_SPEC] * 7,
         out_specs=VMEM_SPEC,
         scratch_shapes=[
-            pltpu.VMEM((5 * SLOTS, 8, LANES), f32),
-            pltpu.SMEM((5 * SLOTS + 8,), i32),
+            pltpu.VMEM((PARTS * SLOTS, 8, LANES), f32),
+            pltpu.SMEM((PARTS * SLOTS + 8,), i32),
         ],
         compiler_params=limit,
         name="moments",

time: 58.2 us -> 48.3 us (0.83)
  the two profiles are of different devices: /device:TPU:0 before, /device:TPU:25 now
where the time goes in v1:
time: 48.3 us; the launch traced here: 47.5 us
  Pallas kernels  19.5 us (40%)
  starting transfers between devices  18.4 us (38%)
  waiting for transfers between devices  7.21 us (15%)
  local copies, waits for them, and re-layouts  1.36 us (3%)
  between operations  0.76 us (2%)
    pallas_call x1, Pallas kernels, per_device(): pl.pallas_call(fit_kernel, out_shape=(out((1024, LANES)), out((BLK * 5, 1...  15.7 us
    ppermute x2, starting transfers between devices, trade(): far_same = lax.ppermute(value, 'sfc', far)  13 us
    ppermute x2, waiting for transfers between devices, trade(): far_same = lax.ppermute(value, 'sfc', far)  5.38 us
    pallas_call x1, Pallas kernels, per_device(): pl.pallas_call(pack_kernel, out_shape=out((49, 8, LANES)), in_specs=[pl.B...  1.93 us
    ppermute x2, starting transfers between devices, trade(): far_other = lax.ppermute(far_same, 'sfc', inside)  1.83 us
    ppermute x2, waiting for transfers between devices, trade(): far_other = lax.ppermute(far_same, 'sfc', inside)  1.81 us
    pallas_call x1, Pallas kernels, per_device(): pl.pallas_call(moment_kernel, out_shape=out((BLK * 6 * 4, LANES)), in_spe...  1.81 us
    ppermute x2, starting transfers between devices, trade(): near_same = lax.ppermute(value, 'sfc', near)  1.23 us
  transfers between devices with their start and end apart: 10, of which 4 were waited for; matrix products, arithmetic and copies ran while one was open for 1% of the time, Pallas kernels for 0%

profile of v1, /device:TPU:25, one launch (start us, length us, event | category | flops | bytes accessed | tf_op | source)
XLA Modules:
  0.0 47.5 jit_solution(4722214687036737404)
XLA Ops:
  0.7 1.9 %pack.1.own_ref = f32[49,8,128]{2,1,0:T(8,128)S(1)} custom-call(f32[256,128]{1,0:T(8,128)} %bitcast.51, f32[3,256,128]{2,1,0:T(8,128)} %bitcast.49, s32[4,16]{1,0:T(4,128)} %bitcast.55), custom_call_target="tpu_custom_call" | custom-call | tf_op jit(solution)/shard_map/pack/pallas_call | solution.py:444
  2.6 0.0 copy-start.1
  2.6 0.8 %collective-permute-start = (f32[49,8,128]{2,1,0:T(8,128)S(1)}, f32[49,8,128]{2,1,0:T(8,128)S(1)}, u32[]{:S(2)}, u32[]{:S(2)}) collective-permute-start(f32[49,8,128]{2,1,0:T(8,128)S(1)} %pack.1.own_ref), channel_id=1, source_target_pairs={{0,1},{1,0},{2,3},{3,2},{4,5},{5,4},{6,7},{7,6},{8,9},{9,8},{10,11... | collective-permute-start | bytes 602120 | tf_op jit(solution)/shard_map/ppermute | solution.py:422
  3.4 1.2 %collective-permute-start.1 = (f32[49,8,128]{2,1,0:T(8,128)S(1)}, f32[49,8,128]{2,1,0:T(8,128)S(1)}, u32[]{:S(2)}, u32[]{:S(2)}) collective-permute-start(f32[49,8,128]{2,1,0:T(8,128)S(1)} %pack.1.own_ref), channel_id=1, source_target_pairs={{0,2},{1,3},{2,0},{3,1},{4,6},{5,7},{6,4},{7,5},{8,10},{9,11},{10,... | collective-permute-start | bytes 602120 | tf_op jit(solution)/shard_map/ppermute | solution.py:421
  4.6 7.3 %collective-permute-start.2 = (f32[49,8,128]{2,1,0:T(8,128)S(1)}, f32[49,8,128]{2,1,0:T(8,128)S(1)}, u32[]{:S(2)}, u32[]{:S(2)}) collective-permute-start(f32[49,8,128]{2,1,0:T(8,128)S(1)} %pack.1.own_ref), channel_id=1, source_target_pairs={{0,1},{1,0},{2,4},{3,5},{4,2},{5,3},{6,8},{7,9},{8,6},{9,7},{10,12... | collective-permute-start | bytes 602120 | tf_op jit(solution)/shard_map/ppermute | solution.py:420
  11.9 0.0 copy-done.4
  11.9 0.1 select_clamp_fusion
  12.0 0.1 reshape.135.tbl_ref
  12.1 0.1 copy.10
  12.2 0.1 reshape.136.refine_ref
  12.3 0.0 collective-permute-done.1.r2_ref
  12.3 0.7 %collective-permute-start.3 = (f32[49,8,128]{2,1,0:T(8,128)S(1)}, f32[49,8,128]{2,1,0:T(8,128)S(1)}, u32[]{:S(2)}, u32[]{:S(2)}) collective-permute-start(f32[49,8,128]{2,1,0:T(8,128)S(1)} %collective-permute-done.1.r2_ref), channel_id=1, source_target_pairs={{0,1},{1,0},{2,3},{3,2},{4,5},{5,4},{6,7},{7,6},{8,9},{9,8},{10,11... | collective-permute-start | bytes 602120 | tf_op jit(solution)/shard_map/ppermute | solution.py:424
  13.0 3.9 %collective-permute-done.2.r3_ref = f32[49,8,128]{2,1,0:T(8,128)S(1)} collective-permute-done((f32[49,8,128]{2,1,0:T(8,128)S(1)}, f32[49,8,128]{2,1,0:T(8,128)S(1)}, u32[]{:S(2)}, u32[]{:S(2)}) %collective-permute-start.2) | collective-permute-done | bytes 200736 | tf_op jit(solution)/shard_map/ppermute | solution.py:420
  17.0 0.9 %collective-permute-start.4 = (f32[49,8,128]{2,1,0:T(8,128)S(1)}, f32[49,8,128]{2,1,0:T(8,128)S(1)}, u32[]{:S(2)}, u32[]{:S(2)}) collective-permute-start(f32[49,8,128]{2,1,0:T(8,128)S(1)} %collective-permute-done.2.r3_ref), channel_id=1, source_target_pairs={{0,1},{1,0},{2,3},{3,2},{4,5},{5,4},{6,7},{7,6},{8,9},{9,8},{10,11... | collective-permute-start | bytes 602120 | tf_op jit(solution)/shard_map/ppermute | solution.py:423
  17.8 0.0 collective-permute-done.r1_ref
  17.9 0.0 collective-permute-done.3.r4_ref
  17.9 1.0 %collective-permute-done.4.r5_ref = f32[49,8,128]{2,1,0:T(8,128)S(1)} collective-permute-done((f32[49,8,128]{2,1,0:T(8,128)S(1)}, f32[49,8,128]{2,1,0:T(8,128)S(1)}, u32[]{:S(2)}, u32[]{:S(2)}) %collective-permute-start.4) | collective-permute-done | bytes 200736 | tf_op jit(solution)/shard_map/ppermute | solution.py:423
  18.9 1.0 %copy-done.2 = f32[8,3,4096]{2,0,1:T(8,128)S(1)} copy-done((f32[8,3,4096]{2,0,1:T(8,128)S(1)}, f32[8,3,4096]{2,0,1:T(8,128)}, u32[]{:S(2)}) %copy-start.2) | copy-done | bytes 393240
  19.9 15.7 %fit.1 = (f32[1024,128]{1,0:T(8,128)}, f32[40,16,128]{2,1,0:T(8,128)S(1)}, f32[16,8,128]{2,1,0:T(8,128)S(1)}) custom-call(s32[48]{0:T(128)S(1)} %reshape.135.tbl_ref, s32[32]{0:T(128)S(1)} %reshape.136.refine_ref, f32[49,8,128]{2,1,0:T(8,128)S(1)} %pack.1.own_ref, f32[49,8,128]{2,1,0:T(8,128)S(1)} %collective-permute-done.r1_ref, ...), custom_call_target="tpu_custom_call" | custom-call | tf_op jit(solution)/shard_map/fit/pallas_call | solution.py:479
  35.6 0.4 collective-permute-start.5
  36.0 0.0 collective-permute-start.6
  36.0 5.7 %collective-permute-start.7 = (f32[16,8,128]{2,1,0:T(8,128)S(1)}, f32[16,8,128]{2,1,0:T(8,128)S(1)}, u32[]{:S(2)}, u32[]{:S(2)}) collective-permute-start(f32[16,8,128]{2,1,0:T(8,128)S(1)} %get-tuple-element.7.s0_ref), channel_id=1, source_target_pairs={{0,1},{1,0},{2,4},{3,5},{4,2},{5,3},{6,8},{7,9},{8,6},{9,7},{10,12... | collective-permute-start | bytes 196616 | tf_op jit(solution)/shard_map/ppermute | solution.py:420
  41.8 0.1 and_convert_fusion
  41.8 0.0 collective-permute-done.6.s2_ref
  41.8 0.5 %collective-permute-start.8 = (f32[16,8,128]{2,1,0:T(8,128)S(1)}, f32[16,8,128]{2,1,0:T(8,128)S(1)}, u32[]{:S(2)}, u32[]{:S(2)}) collective-permute-start(f32[16,8,128]{2,1,0:T(8,128)S(1)} %collective-permute-done.6.s2_ref), channel_id=1, source_target_pairs={{0,1},{1,0},{2,3},{3,2},{4,5},{5,4},{6,7},{7,6},{8,9},{9,8},{10,11... | collective-permute-start | bytes 196616 | tf_op jit(solution)/shard_map/ppermute | solution.py:424
  42.3 1.5 %collective-permute-done.7.s3_ref = f32[16,8,128]{2,1,0:T(8,128)S(1)} collective-permute-done((f32[16,8,128]{2,1,0:T(8,128)S(1)}, f32[16,8,128]{2,1,0:T(8,128)S(1)}, u32[]{:S(2)}, u32[]{:S(2)}) %collective-permute-start.7) | collective-permute-done | bytes 65568 | tf_op jit(solution)/shard_map/ppermute | solution.py:420
  43.8 1.0 %collective-permute-start.9 = (f32[16,8,128]{2,1,0:T(8,128)S(1)}, f32[16,8,128]{2,1,0:T(8,128)S(1)}, u32[]{:S(2)}, u32[]{:S(2)}) collective-permute-start(f32[16,8,128]{2,1,0:T(8,128)S(1)} %collective-permute-done.7.s3_ref), channel_id=1, source_target_pairs={{0,1},{1,0},{2,3},{3,2},{4,5},{5,4},{6,7},{7,6},{8,9},{9,8},{10,11... | collective-permute-start | bytes 196616 | tf_op jit(solution)/shard_map/ppermute | solution.py:423
  44.8 0.1 reshape.145.meta_ref
  44.9 0.0 collective-permute-done.5.s1_ref
  44.9 0.0 collective-permute-done.8.s4_ref
  44.9 0.8 %collective-permute-done.9.s5_ref = f32[16,8,128]{2,1,0:T(8,128)S(1)} collective-permute-done((f32[16,8,128]{2,1,0:T(8,128)S(1)}, f32[16,8,128]{2,1,0:T(8,128)S(1)}, u32[]{:S(2)}, u32[]{:S(2)}) %collective-permute-start.9) | collective-permute-done | bytes 65568 | tf_op jit(solution)/shard_map/ppermute | solution.py:423
  45.6 1.8 %moments.1 = f32[192,128]{1,0:T(8,128)} custom-call(s32[384]{0:T(512)S(1)} %reshape.145.meta_ref, f32[40,16,128]{2,1,0:T(8,128)S(1)} %get-tuple-element.6.pf_ref, f32[16,8,128]{2,1,0:T(8,128)S(1)} %get-tuple-element.7.s0_ref, f32[16,8,128]{2,1,0:T(8,128)S(1)} %collective-permute-done.5.s1_ref, f32[16,8,128]{2,1,0:T(8,128)S(1)} %collective-permute-done.6.s2_ref, ...), custom_call_target="tpu_custom_call" | custom-call | tf_op jit(solution)/shard_map/moments/pallas_call | solution.py:513
  (21 shorter events, 0.2 us)
Async XLA Ops:
  0.6 11.3 %copy-start.4 = (s32[8,6]{1,0:T(8,128)S(1)}, s32[8,6]{1,0:T(8,128)}, u32[]{:S(2)}) copy-start(s32[8,6]{1,0:T(8,128)} %param.8) | copy-start | bytes 580
  0.6 11.4 %copy-start.3 = (s32[16,4]{0,1:T(4,128)S(1)}, s32[16,4]{0,1:T(4,128)}, u32[]{:S(2)}) copy-start(s32[16,4]{0,1:T(4,128)} %param.9) | copy-start | bytes 772
  0.7 18.3 %copy-start = (f32[8,3,4096]{2,0,1:T(8,128)S(1)}, f32[8,3,4096]{2,0,1:T(8,128)}, u32[]{:S(2)}) copy-start(f32[8,3,4096]{2,0,1:T(8,128)} %param.6) | copy-start | bytes 1179652
  2.6 16.3 %copy-start.1 = (f32[8,4096]{1,0:T(8,128)S(1)}, f32[8,4096]{1,0:T(8,128)}, u32[]{:S(2)}) copy-start(f32[8,4096]{1,0:T(8,128)} %param.5) | copy-start | bytes 393220
  2.6 15.2 %collective-permute-start = (f32[49,8,128]{2,1,0:T(8,128)S(1)}, f32[49,8,128]{2,1,0:T(8,128)S(1)}, u32[]{:S(2)}, u32[]{:S(2)}) collective-permute-start(f32[49,8,128]{2,1,0:T(8,128)S(1)} %pack.1.own_ref), channel_id=1, source_target_pairs={{0,1},{1,0},{2,3},{3,2},{4,5},{5,4},{6,7},{7,6},{8,9},{9,8},{10,11... | collective-permute-start | bytes 602120 | tf_op jit(solution)/shard_map/ppermute | solution.py:422
  3.4 8.9 %collective-permute-start.1 = (f32[49,8,128]{2,1,0:T(8,128)S(1)}, f32[49,8,128]{2,1,0:T(8,128)S(1)}, u32[]{:S(2)}, u32[]{:S(2)}) collective-permute-start(f32[49,8,128]{2,1,0:T(8,128)S(1)} %pack.1.own_ref), channel_id=1, source_target_pairs={{0,2},{1,3},{2,0},{3,1},{4,6},{5,7},{6,4},{7,5},{8,10},{9,11},{10,... | collective-permute-start | bytes 602120 | tf_op jit(solution)/shard_map/ppermute | solution.py:421
  4.6 12.4 %collective-permute-start.2 = (f32[49,8,128]{2,1,0:T(8,128)S(1)}, f32[49,8,128]{2,1,0:T(8,128)S(1)}, u32[]{:S(2)}, u32[]{:S(2)}) collective-permute-start(f32[49,8,128]{2,1,0:T(8,128)S(1)} %pack.1.own_ref), channel_id=1, source_target_pairs={{0,1},{1,0},{2,4},{3,5},{4,2},{5,3},{6,8},{7,9},{8,6},{9,7},{10,12... | collective-permute-start | bytes 602120 | tf_op jit(solution)/shard_map/ppermute | solution.py:420
  12.3 5.6 %collective-permute-start.3 = (f32[49,8,128]{2,1,0:T(8,128)S(1)}, f32[49,8,128]{2,1,0:T(8,128)S(1)}, u32[]{:S(2)}, u32[]{:S(2)}) collective-permute-start(f32[49,8,128]{2,1,0:T(8,128)S(1)} %collective-permute-done.1.r2_ref), channel_id=1, source_target_pairs={{0,1},{1,0},{2,3},{3,2},{4,5},{5,4},{6,7},{7,6},{8,9},{9,8},{10,11... | collective-permute-start | bytes 602120 | tf_op jit(solution)/shard_map/ppermute | solution.py:424
  17.0 1.9 %collective-permute-start.4 = (f32[49,8,128]{2,1,0:T(8,128)S(1)}, f32[49,8,128]{2,1,0:T(8,128)S(1)}, u32[]{:S(2)}, u32[]{:S(2)}) collective-permute-start(f32[49,8,128]{2,1,0:T(8,128)S(1)} %collective-permute-done.2.r3_ref), channel_id=1, source_target_pairs={{0,1},{1,0},{2,3},{3,2},{4,5},{5,4},{6,7},{7,6},{8,9},{9,8},{10,11... | collective-permute-start | bytes 602120 | tf_op jit(solution)/shard_map/ppermute | solution.py:423
  18.9 1.0 %copy-start.2 = (f32[8,3,4096]{2,0,1:T(8,128)S(1)}, f32[8,3,4096]{2,0,1:T(8,128)}, u32[]{:S(2)}) copy-start(f32[8,3,4096]{2,0,1:T(8,128)} %param.7) | copy-start | bytes 1179652
  35.6 9.2 %collective-permute-start.5 = (f32[16,8,128]{2,1,0:T(8,128)S(1)}, f32[16,8,128]{2,1,0:T(8,128)S(1)}, u32[]{:S(2)}, u32[]{:S(2)}) collective-permute-start(f32[16,8,128]{2,1,0:T(8,128)S(1)} %get-tuple-element.7.s0_ref), channel_id=1, source_target_pairs={{0,1},{1,0},{2,3},{3,2},{4,5},{5,4},{6,7},{7,6},{8,9},{9,8},{10,11... | collective-permute-start | bytes 196616 | tf_op jit(solution)/shard_map/ppermute | solution.py:422
  36.0 5.8 %collective-permute-start.6 = (f32[16,8,128]{2,1,0:T(8,128)S(1)}, f32[16,8,128]{2,1,0:T(8,128)S(1)}, u32[]{:S(2)}, u32[]{:S(2)}) collective-permute-start(f32[16,8,128]{2,1,0:T(8,128)S(1)} %get-tuple-element.7.s0_ref), channel_id=1, source_target_pairs={{0,2},{1,3},{2,0},{3,1},{4,6},{5,7},{6,4},{7,5},{8,10},{9,11},{10,... | collective-permute-start | bytes 196616 | tf_op jit(solution)/shard_map/ppermute | solution.py:421
  36.0 7.8 %collective-permute-start.7 = (f32[16,8,128]{2,1,0:T(8,128)S(1)}, f32[16,8,128]{2,1,0:T(8,128)S(1)}, u32[]{:S(2)}, u32[]{:S(2)}) collective-permute-start(f32[16,8,128]{2,1,0:T(8,128)S(1)} %get-tuple-element.7.s0_ref), channel_id=1, source_target_pairs={{0,1},{1,0},{2,4},{3,5},{4,2},{5,3},{6,8},{7,9},{8,6},{9,7},{10,12... | collective-permute-start | bytes 196616 | tf_op jit(solution)/shard_map/ppermute | solution.py:420
  41.8 3.0 %collective-permute-start.8 = (f32[16,8,128]{2,1,0:T(8,128)S(1)}, f32[16,8,128]{2,1,0:T(8,128)S(1)}, u32[]{:S(2)}, u32[]{:S(2)}) collective-permute-start(f32[16,8,128]{2,1,0:T(8,128)S(1)} %collective-permute-done.6.s2_ref), channel_id=1, source_target_pairs={{0,1},{1,0},{2,3},{3,2},{4,5},{5,4},{6,7},{7,6},{8,9},{9,8},{10,11... | collective-permute-start | bytes 196616 | tf_op jit(solution)/shard_map/ppermute | solution.py:424
  43.8 1.9 %collective-permute-start.9 = (f32[16,8,128]{2,1,0:T(8,128)S(1)}, f32[16,8,128]{2,1,0:T(8,128)S(1)}, u32[]{:S(2)}, u32[]{:S(2)}) collective-permute-start(f32[16,8,128]{2,1,0:T(8,128)S(1)} %collective-permute-done.7.s3_ref), channel_id=1, source_target_pairs={{0,1},{1,0},{2,3},{3,2},{4,5},{5,4},{6,7},{7,6},{8,9},{9,8},{10,11... | collective-permute-start | bytes 196616 | tf_op jit(solution)/shard_map/ppermute | solution.py:423

commit v2 on v1

v2 whole, which is shorter than its diff:
```python
import functools

import jax
import jax.numpy as jnp
from jax import lax
from jax.experimental import pallas as pl
from jax.experimental.pallas import tpu as pltpu
from jax.sharding import PartitionSpec as P

BLK = 8
SLOTS = 16
PARTS = 6
TODO = 112
PASSES = 6
LANES = 128
NODES = (0.5 - 3.0**0.5 / 6.0, 0.5 + 3.0**0.5 / 6.0)
TIME_STEP = 0.25
DAMPING = 0.1
VMEM_SPEC = pl.BlockSpec(memory_space=pltpu.VMEM)
SMEM_SPEC = pl.BlockSpec(memory_space=pltpu.SMEM)


def lane_ids():
    return lax.broadcasted_iota(jnp.int32, (8, LANES), 1)


def row_ids():
    return lax.broadcasted_iota(jnp.int32, (8, LANES), 0)


def pick(values, index):
    return jnp.take_along_axis(values, index, axis=1, mode="promise_in_bounds")


def cells(ref, b, xh, yh):
    return ref[pl.ds(xh * 128 + yh * 8 + b, 8, stride=16), :]


def side_index(lane):
    l = lane % 64
    index = jnp.where(l < 16, l, jnp.where(l < 32, l + 96, 16 * (l % 8) + jnp.where(l < 48, 0, 15)))
    upper = ((l >= 16) & (l < 32)) | ((l >= 40) & (l < 48)) | (l >= 56)
    return index, upper


def pack_kernel(
    frac_hbm, cent_hbm, refine_hbm, near_hbm, out_ref, field, refine_ref, near_ref, sems
):
    copies = [
        pltpu.make_async_copy(frac_hbm if f == 0 else cent_hbm.at[f - 1], field.at[f], sems.at[f])
        for f in range(4)
    ]
    copies.append(pltpu.make_async_copy(refine_hbm, refine_ref, sems.at[4]))
    copies.append(pltpu.make_async_copy(near_hbm, near_ref, sems.at[5]))
    for copy in copies:
        copy.start()
    lane = lane_ids()
    index, upper = side_index(lane)
    out_ref[48] = jnp.zeros((8, LANES), jnp.float32)
    for copy in copies:
        copy.wait()
    out_ref[48, 0:4, 0:SLOTS] = refine_ref[...].astype(jnp.float32)

    def block(b, carry):
        for xh in (0, 1):
            sides = []
            for f in range(4):
                half = [cells(field.at[f], b, xh, yh) for yh in (0, 1)]
                for yh in (0, 1):
                    row = half[yh][0:1] if xh == 0 else half[yh][7:8]
                    out_ref[b * 6 + xh, 2 * f + yh : 2 * f + yh + 1, :] = row
                sides.append(jnp.where(upper, pick(half[1], index), pick(half[0], index)))
            for fp in (0, 1):
                out_ref[b * 6 + 2 + 2 * fp + xh] = jnp.where(lane < 64, sides[2 * fp], sides[2 * fp + 1])
        return carry

    lax.fori_loop(0, BLK, block, 0)


def solve(h, g):
    a, b, c = h[0][0], h[0][1], h[1][1]
    ra = 1.0 / (a * c - b * b)
    ia, ib, ic = c * ra, b * ra, a * ra
    p, q, r, s = h[0][2], h[0][3], h[1][2], h[1][3]
    wp, wq = ia * p - ib * r, ia * q - ib * s
    wr, ws = ic * r - ib * p, ic * s - ib * q
    sa = h[2][2] - p * wp - r * wr
    sb = h[2][3] - p * wq - r * ws
    sc = h[3][3] - q * wq - s * ws
    z0, z1 = ia * g[0] - ib * g[1], ic * g[1] - ib * g[0]
    y0 = g[2] - p * z0 - r * z1
    y1 = g[3] - q * z0 - s * z1
    rs = 1.0 / (sa * sc - sb * sb)
    x2 = (sc * y0 - sb * y1) * rs
    x3 = (sa * y1 - sb * y0) * rs
    return z0 - wp * x2 - wq * x3, z1 - wr * x2 - ws * x3, x2, x3


def one_pass(load, params):
    a, b, c, d = params
    h = [[None] * 4 for _ in range(4)]
    g = [None] * 4

    def add(total, value):
        return value if total is None else total + value

    for j in range(7):
        px, py, pz, q = load(j)
        t = jnp.tanh(a * px + b * py + c * pz + d)
        s = 1.0 - t * t
        w = s * s
        r = s * (t + q)
        wx, wy, wz = w * px, w * py, w * pz
        h[0][0] = add(h[0][0], wx * px)
        h[0][1] = add(h[0][1], wx * py)
        h[0][2] = add(h[0][2], wx * pz)
        h[0][3] = add(h[0][3], wx)
        h[1][1] = add(h[1][1], wy * py)
        h[1][2] = add(h[1][2], wy * pz)
        h[1][3] = add(h[1][3], wy)
        h[2][2] = add(h[2][2], wz * pz)
        h[2][3] = add(h[2][3], wz)
        h[3][3] = add(h[3][3], w)
        g[0] = add(g[0], r * px)
        g[1] = add(g[1], r * py)
        g[2] = add(g[2], r * pz)
        g[3] = add(g[3], r)
    for i in range(4):
        h[i][i] = h[i][i] + 4.0 * DAMPING
    step = solve(h, g)
    return tuple(p - u for p, u in zip(params, step))


def start(load):
    f = [0.5 - 0.5 * load(j)[3] for j in range(7)]
    cx, cy, cz, _ = load(0)
    a, b, c = (2.0 * (f[2 * k + 2] - f[2 * k + 1]) for k in range(3))
    d = 2.0 * (2.0 * f[0] - 1.0) - a * cx - b * cy - c * cz
    return a, b, c, d


def held_as(f, j, value):
    if f == 0:
        return 1.0 - 2.0 * value
    if j > 0 and (j - 1) // 2 == f - 1:
        return value + (1.0 if (j - 1) % 2 else -1.0)
    return value


def own_points(field, xpad, st):
    lane = lane_ids()

    def block(b, carry):
        for f in range(4):

            def put(j, xh, yh, value):
                at = pl.ds(b * 32 + yh * 16 + xh * 8, 8)
                st[j, (f + 3) % 4, at, :] = held_as(f, j, value)

            own = [[cells(field.at[f], b, xh, yh) for yh in (0, 1)] for xh in (0, 1)]
            for yh in (0, 1):
                for xh in (0, 1):
                    xpad[f, yh, 8 + 8 * xh : 16 + 8 * xh, :] = own[xh][yh]
            for xh in (0, 1):
                up = [pltpu.roll(own[xh][yh], 16, 1) for yh in (0, 1)]
                down = [pltpu.roll(own[xh][yh], LANES - 16, 1) for yh in (0, 1)]
                for yh in (0, 1):
                    mine = own[xh][yh]
                    put(0, xh, yh, mine)
                    put(1, xh, yh, xpad[f, yh, 7 + 8 * xh : 15 + 8 * xh, :])
                    put(2, xh, yh, xpad[f, yh, 9 + 8 * xh : 17 + 8 * xh, :])
                    put(3, xh, yh, up[0] if yh == 0 else jnp.where(lane < 16, up[0], up[1]))
                    put(4, xh, yh, down[1] if yh == 1 else jnp.where(lane >= 112, down[1], down[0]))
                    put(5, xh, yh, pltpu.roll(mine, 1, 1))
                    put(6, xh, yh, pltpu.roll(mine, LANES - 1, 1))
        return carry

    xpad[...] = jnp.zeros_like(xpad)
    lax.fori_loop(0, BLK, block, 0)


def patch(b, tbl_ref, table, st):
    lane = lane_ids()
    group = (lane % 64) // 16
    src = [tbl_ref[b * 6 + k] for k in range(6)]
    low, high = table[src[0]], table[src[1]]

    def put(j, f, at, mask, value):
        c = (f + 3) % 4
        st[j, c, at, :] = jnp.where(mask, held_as(f, j, value), st[j, c, at, :])

    for f in range(4):
        c = (f + 3) % 4
        for yh in (0, 1):
            row = b * 32 + yh * 16
            st[1, c, row : row + 1, :] = held_as(f, 1, low[2 * f + yh : 2 * f + yh + 1])
            st[2, c, row + 15 : row + 16, :] = held_as(f, 2, high[2 * f + yh : 2 * f + yh + 1])
    for fp in (0, 1):
        for xh in (0, 1):
            ghost = [table[src[k] + 2 * fp + xh] for k in range(2, 6)]
            mixed = jnp.where(
                group < 2,
                jnp.where(group == 0, ghost[1], ghost[0]),
                jnp.where(group == 2, ghost[3], ghost[2]),
            )
            for fh in (0, 1):
                f = 2 * fp + fh
                for yh in (0, 1):
                    row = b * 32 + yh * 16 + xh * 8
                    at = slice(row, row + 8)
                    index = fh * 64 + jnp.where(lane % 16 == 15, 32, 48) + yh * 8 + lane // 16
                    value = pick(mixed, index)
                    put(5, f, at, lane % 16 == 0, value)
                    put(6, f, at, lane % 16 == 15, value)
                    value = pick(mixed, fh * 64 + (16 if yh == 0 else 0) + lane % 16)
                    if yh == 0:
                        put(3, f, at, lane < 16, value)
                    else:
                        put(4, f, at, lane >= 112, value)


def face_index(lane):
    index = jnp.where(
        lane < 48,
        lane % 16,
        jnp.where(lane < 64, lane + 64, 16 * (lane % 8) + jnp.where(lane < 80, 0, 15)),
    )
    upper = (
        ((lane >= 48) & (lane < 64)) | ((lane >= 72) & (lane < 80)) | ((lane >= 88) & (lane < 96))
    )
    return index, upper


def x_faces(lane, row, first, h):
    unroll_x = row * 16 + lane % 16
    low = pick(jnp.broadcast_to(first[0][h][0:1], (8, LANES)), unroll_x)
    high = pick(jnp.broadcast_to(first[1][h][7:8], (8, LANES)), unroll_x)
    return low, high


def prepare_kernel(field, velo_ref, points_hbm, out_ref, xpad, st, sem):
    own_points(field, xpad, st)
    keep = pltpu.make_async_copy(st, points_hbm, sem)
    keep.start()
    lane, row = lane_ids(), row_ids()
    index, upper = face_index(lane)

    def block(b, carry):
        x, y, z = (
            [[cells(velo_ref.at[axis], b, xh, yh) for yh in (0, 1)] for xh in (0, 1)]
            for axis in range(3)
        )
        for h in (0, 1):
            low, high = x_faces(lane, row, x, h)
            y_sides = jnp.where(upper, pick(y[h][1], index), pick(y[h][0], index))
            z_sides = jnp.where(upper, pick(z[h][1], index), pick(z[h][0], index))
            sides = jnp.where(lane < 64, y_sides, z_sides)
            out_ref[b, 8 * h : 8 * h + 8, :] = jnp.where(
                lane < 16, low, jnp.where(lane < 32, high, sides)
            )
        return carry

    lax.fori_loop(0, BLK, block, 0, unroll=2)
    keep.wait()


def plane_faces(params, pf, count, first):
    lane, row = lane_ids(), row_ids()
    index, upper = face_index(lane)

    def block(b, carry):
        for comp in range(4):
            value = [
                [params[comp, pl.ds(b * 32 + yh * 16 + xh * 8, 8), :] for yh in (0, 1)]
                for xh in (0, 1)
            ]
            for h in (0, 1):
                low, high = x_faces(lane, row, value, h)
                sides = jnp.where(upper, pick(value[h][1], index), pick(value[h][0], index))
                pf[(first + b) * 4 + comp, 8 * h : 8 * h + 8, :] = jnp.where(
                    lane < 16, low, jnp.where(lane < 32, high, sides)
                )
        return carry

    lax.fori_loop(0, count, block, 0, unroll=2)


def fine_slots(refine_ref, params, speed_ref, slots_ref):
    lane, row = lane_ids(), row_ids()
    isub = (lane // 16) % 2
    odd = isub == 1
    second = 2 * (lane % 8) + (lane // 8) % 2
    x_source = 16 * ((2 * row + isub) % 8) + second

    def tile(g, carry):
        total = [None] * 3
        for q in range(4):
            f = refine_ref[2 * (4 * g + q)]
            k = refine_ref[2 * (4 * g + q) + 1]
            axis = lax.shift_right_logical(k, 1)
            side = k & 1
            y_source = side * 112 + second
            z_source = 16 * (second % 8) + 15 * side
            is_x = jnp.full((8, LANES), axis, jnp.int32) == 0
            is_y = jnp.full((8, LANES), axis, jnp.int32) == 1
            upper = second >= 8
            got = []
            for comp in (axis, 3):
                at = f * 32
                ref = params.at[comp]
                line = at + side * 15
                x_value = pick(
                    jnp.where(
                        row < 4,
                        jnp.broadcast_to(ref[pl.ds(line, 1), :], (8, LANES)),
                        jnp.broadcast_to(ref[pl.ds(line + 16, 1), :], (8, LANES)),
                    ),
                    x_source,
                )
                part = [
                    [ref[pl.ds(at + 16 * yh + sub, 8, stride=2), :] for yh in (0, 1)]
                    for sub in (0, 1)
                ]
                high_side = jnp.full((8, LANES), side, jnp.int32) == 1
                y_part = [pick(jnp.where(high_side, p[1], p[0]), y_source) for p in part]
                z_part = [jnp.where(upper, pick(p[1], z_source), pick(p[0], z_source)) for p in part]
                got.append(
                    jnp.where(
                        is_x,
                        x_value,
                        jnp.where(
                            is_y,
                            jnp.where(odd, y_part[1], y_part[0]),
                            jnp.where(odd, z_part[1], z_part[0]),
                        ),
                    )
                )
            index = k * 16 + second
            got.append(
                jnp.where(
                    odd,
                    pick(speed_ref[f, pl.ds(1, 8, stride=2), :], index),
                    pick(speed_ref[f, pl.ds(0, 8, stride=2), :], index),
                )
            )
            for comp in range(3):
                old = total[comp]
                total[comp] = got[comp] if q == 0 else jnp.where(lane // 32 == q, got[comp], old)
        for comp in range(3):
            slots_ref[4 * comp + g] = total[comp]
        return carry

    lax.fori_loop(0, SLOTS // 4, tile, 0)


def fit_kernel(
    tbl_ref, refine_ref, own_ref, r1_ref, r2_ref, r3_ref, r4_ref, r5_ref, points_hbm, speed_ref,
    params, slots_ref, st, table, sems,
):
    fetches = [
        pltpu.make_async_copy(
            points_hbm.at[:, :, pl.ds(b * 32, 32), :], st.at[:, :, pl.ds(b * 32, 32), :], sems.at[b]
        )
        for b in range(BLK)
    ]
    for fetch in fetches:
        fetch.start()
    lane = lane_ids()
    for at, ref in enumerate((own_ref, r1_ref, r2_ref, r3_ref, r4_ref, r5_ref)):

        def copy(i, carry, at=at, ref=ref):
            for u in range(12):
                table[at * 48 + i * 12 + u] = ref[i * 12 + u]
            return carry

        lax.fori_loop(0, 4, copy, 0)

    def swap(i, carry):
        for u in range(2, 6):
            v = own_ref[i * 6 + u]
            odd = (lane // 16) % 2 == 1
            table[288 + i * 6 + u] = jnp.where(
                odd, pltpu.roll(v, 16, 1), pltpu.roll(v, LANES - 16, 1)
            )
        return carry

    lax.fori_loop(0, BLK, swap, 0, unroll=2)
    for b in range(BLK):
        fetches[b].wait()
        patch(b, tbl_ref, table, st)
        at = slice(b * 32, b * 32 + 32)

        def load(j, at=at):
            return tuple(st[j, c, at, :] for c in range(4))

        values = lax.fori_loop(0, PASSES, lambda _, p, load=load: one_pass(load, p), start(load))
        for comp in range(4):
            params[comp, at, :] = values[comp]
    fine_slots(refine_ref, params, speed_ref, slots_ref)


def emit_kernel(meta_ref, params, planes_hbm, pf_ref, todo_ref, buffer, sem):
    def emit(b, carry):
        for comp in range(4):
            for xh in (0, 1):
                for yh in (0, 1):
                    buffer[pl.ds(b * 128 + 64 * xh + 4 * yh + comp, 8, stride=8), :] = params[
                        comp, pl.ds(b * 32 + yh * 16 + xh * 8, 8), :
                    ]
        return carry

    lax.fori_loop(0, BLK, emit, 0)
    copy = pltpu.make_async_copy(buffer, planes_hbm, sem)
    copy.start()
    plane_faces(params, pf_ref, BLK, 0)

    def collect(i, n):
        todo_ref[n] = i
        return n + meta_ref[i]

    count = lax.fori_loop(0, PARTS * SLOTS, collect, 0, unroll=8)
    for extra in range(4):
        todo_ref[count + extra] = 0
    todo_ref[TODO - 1] = count
    copy.wait()


def moment_kernel(
    meta_ref, todo, pf_ref, speed_ref, s0_ref, s1_ref, s2_ref, s3_ref, s4_ref, s5_ref, out_ref, slots
):
    lane = lane_ids()
    row = row_ids()
    out_ref[...] = jnp.zeros_like(out_ref)
    for at, ref in enumerate((s0_ref, s1_ref, s2_ref, s3_ref, s4_ref, s5_ref)):
        for u in range(12):
            slots[at * 12 + u] = ref[u]
    total = PARTS * SLOTS

    count = todo[TODO - 1]
    quarter = lane // 32
    first_off = (((lane // 16) % 2).astype(jnp.float32) - 0.5) * 0.5
    second_off = (((lane // 8) % 2).astype(jnp.float32) - 0.5) * 0.5

    def group(g, carry):
        fine = [None] * 3
        coarse = [None] * 5
        sign = None
        weight = None
        where = []

        def merge(old, new, q):
            return new if old is None else jnp.where(quarter == q, new, old)

        for q in range(4):
            at = 4 * g + q
            i = todo[at]
            c = meta_ref[total + i]
            k = meta_ref[2 * total + i]
            quad = meta_ref[3 * total + i]
            axis = lax.shift_right_logical(k, 1)
            qa = lax.shift_right_logical(quad, 1)
            qb = quad & 1
            held = lax.shift_right_logical(i, 4) * 12 + (lax.shift_right_logical(i, 2) & 3)
            turn = (i & 3) * 32 + lane % 32
            for comp in range(3):
                fine[comp] = merge(fine[comp], pick(slots[held + 4 * comp], turn), q)
            index = k * 16 + qb * 8 + lane % 8
            which = (axis, jnp.where(axis == 0, 1, 0), jnp.where(axis == 2, 1, 2), 3, 4)
            for at_comp, comp in enumerate(which):
                rows_at = pl.ds(pl.multiple_of(qa * 8, 8), 8)
                value = speed_ref[c, rows_at, :] if at_comp == 4 else pf_ref[c * 4 + comp, rows_at, :]
                coarse[at_comp] = merge(coarse[at_comp], pick(value, index), q)
            s = jnp.where((k & 1) == 1, -1.0, 1.0).astype(jnp.float32)
            sign = merge(sign, jnp.full((8, LANES), s, jnp.float32), q)
            on = jnp.where(at < count, 1.0, 0.0).astype(jnp.float32)
            weight = merge(weight, jnp.full((8, LANES), on, jnp.float32), q)
            where.append((((c * 6 + k) * 2 + qa) * 2, qb))
        an, df, uf = fine
        cn, t1, t2, dc, uc = coarse
        speed = sign * 0.5 * (uf + uc)
        depth = jnp.abs(speed) * TIME_STEP
        outflow = jnp.maximum(speed, 0.0)
        inflow = jnp.minimum(speed, 0.0)
        base = t1 * first_off + t2 * second_off + dc
        volume = 0.0
        moment = 0.0
        for node in NODES:
            fine_phase = an * (sign * (0.5 - node * depth)) + df
            coarse_phase = cn * (-sign * (0.5 - 0.5 * node * depth)) + base
            fine_model = 0.5 * (1.0 + jnp.tanh(fine_phase))
            coarse_model = 0.5 * (1.0 + jnp.tanh(coarse_phase))
            gain = outflow * fine_model
            loss = inflow * coarse_model
            volume = volume + 0.5 * TIME_STEP * (gain + loss)
            moment = moment + 0.5 * TIME_STEP * node * depth * sign * (loss - gain)
        sums = []
        for value in (volume * weight, moment * weight):
            value = value + pltpu.roll(value, LANES - 8, 1)
            sums.append(value + pltpu.roll(value, LANES - 16, 1))
        for q in range(4):
            target, qb = where[q]
            index = 32 * q + lane % 8
            keep = (lane // 16 == row) & ((lane // 8) % 2 == qb)
            rows = [
                jnp.sum(jnp.where(keep, pick(value, index), 0.0), axis=0, keepdims=True)
                for value in sums
            ]
            for m in range(2):
                out_ref[pl.ds(target + m, 1), :] = out_ref[pl.ds(target + m, 1), :] + rows[m]
        return carry

    lax.fori_loop(0, (count + 3) // 4, group, 0)


def partners(n, distance, offset):
    pairs = []
    for i in range(n):
        up = ((i - offset) // distance) % 2 == 0
        j = i + distance if up else i - distance
        pairs.append((i, j if 0 <= j < n else i ^ 1))
    return pairs


def trade(value):
    n = lax.axis_size("sfc")
    far = lax.ppermute(value, "sfc", partners(n, 2, 2))
    near = lax.ppermute(value, "sfc", partners(n, 2, 0))
    return [lax.ppermute(value, "sfc", partners(n, 1, 0)), near, far]


def relay(values):
    inside = partners(lax.axis_size("sfc"), 1, 0)
    return [lax.ppermute(value, "sfc", inside) for value in values]


def tiles(field):
    return field.reshape(BLK, 32, LANES).transpose(1, 0, 2).reshape(256, LANES)


def tiles3(field):
    return field.reshape(BLK, 3, 32, LANES).transpose(1, 2, 0, 3).reshape(3, 256, LANES)


def lasting(microseconds):
    return pl.CostEstimate(flops=0, transcendentals=0, bytes_accessed=microseconds * 3_500_000)


def per_device(fraction, centroid, velocity, neighbours, refinement):
    f32 = jnp.float32
    i32 = jnp.int32
    me = lax.axis_index("sfc").astype(i32)
    frac, cent, velo = tiles(fraction), tiles3(centroid), tiles3(velocity)
    out = functools.partial(jax.ShapeDtypeStruct, dtype=f32)
    limit = pltpu.CompilerParams(vmem_limit_bytes=12 << 20)

    hbm = pl.BlockSpec(memory_space=pltpu.HBM)
    faces, field, fine_rows, neighbours = pl.pallas_call(
        pack_kernel,
        out_shape=(
            out((49, 8, LANES)),
            out((4, 256, LANES)),
            jax.ShapeDtypeStruct((4, SLOTS), i32),
            jax.ShapeDtypeStruct((BLK, 6), i32),
        ),
        in_specs=[hbm] * 4,
        out_specs=(VMEM_SPEC,) * 4,
        scratch_shapes=[pltpu.SemaphoreType.DMA((6,))],
        compiler_params=limit,
        name="pack",
    )(*(pltpu.with_memory_space_constraint(v, pltpu.HBM) for v in (frac, cent, refinement.T, neighbours)))
    got = trade(faces)
    got = got + relay(got[1:])

    device = neighbours // BLK
    step = device // 2 - me // 2
    near_step = 1 - 2 * ((me // 2) % 2)
    part = jnp.where(
        step == 0,
        jnp.where(device == me, 0, 1),
        jnp.where(step == near_step, 2, 3) + jnp.where(device % 2 == me % 2, 0, 2),
    )
    direction = jnp.arange(6, dtype=i32)[None, :]
    block = jnp.arange(BLK, dtype=i32)[:, None]
    inside = part * BLK + neighbours % BLK
    x_row = jnp.where(neighbours >= 0, inside * 6 + 1 - direction, block * 6 + direction)
    yz_row = jnp.where(neighbours >= 0, inside, 48 + block) * 6 + 2
    rows = jnp.where(direction < 2, x_row, yz_row)
    rows = jnp.clip(rows, 0, 333).reshape(48)

    fine_local = jnp.clip(fine_rows[0] - me * BLK, 0, BLK - 1)
    fine_side = jnp.clip(fine_rows[1], 0, 5)
    fine_table = jnp.stack([fine_local, fine_side], axis=1).reshape(2 * SLOTS)

    points, speed = pl.pallas_call(
        prepare_kernel,
        out_shape=(pltpu.HBM((7, 4, 256, LANES), f32), out((BLK, 16, LANES))),
        in_specs=[VMEM_SPEC] * 2,
        out_specs=(hbm, VMEM_SPEC),
        scratch_shapes=[
            pltpu.VMEM((4, 2, 32, LANES), f32),
            pltpu.VMEM((7, 4, 256, LANES), f32),
            pltpu.SemaphoreType.DMA,
        ],
        compiler_params=limit,
        cost_estimate=lasting(4),
        name="prepare",
    )(field, velo)
    points = pltpu.with_memory_space_constraint(points, pltpu.HBM)
    params, slots = pl.pallas_call(
        fit_kernel,
        out_shape=(out((4, 256, LANES)), out((12, 8, LANES))),
        in_specs=[SMEM_SPEC] * 2 + [VMEM_SPEC] * 6 + [hbm, VMEM_SPEC],
        out_specs=(VMEM_SPEC,) * 2,
        scratch_shapes=[
            pltpu.VMEM((7, 4, 256, LANES), f32),
            pltpu.VMEM((336, 8, LANES), f32),
            pltpu.SemaphoreType.DMA((BLK,)),
        ],
        compiler_params=limit,
        cost_estimate=lasting(12),
        name="fit",
    )(rows, fine_table, faces, *got, points, speed)
    got_slots = trade(slots)

    count = lax.axis_size("sfc")
    twice = (me // 2 == 0) | (me // 2 == count // 2 - 1)
    tables = jnp.stack(
        [fine_rows] + [v[48, 0:4, 0:SLOTS].astype(i32) for v in got], axis=1
    )
    part_ids = jnp.arange(PARTS, dtype=i32)[:, None]
    fresh = jnp.logical_not(twice & ((part_ids == 3) | (part_ids == 5)))
    mine = (tables[0] >= 0) & (tables[2] // BLK == me) & fresh
    side = jnp.clip(tables[1], 0, 5)
    meta = jnp.stack(
        [
            mine.astype(i32),
            jnp.clip(tables[2], 0, None) % BLK,
            side + 1 - 2 * (side % 2),
            jnp.clip(tables[3], 0, 3),
        ]
    ).reshape(4 * PARTS * SLOTS)

    planes, plane_face, todo = pl.pallas_call(
        emit_kernel,
        out_shape=(
            out((1024, LANES)),
            out((BLK * 4, 16, LANES)),
            jax.ShapeDtypeStruct((TODO,), i32),
        ),
        in_specs=[SMEM_SPEC, VMEM_SPEC],
        out_specs=(hbm, VMEM_SPEC, SMEM_SPEC),
        scratch_shapes=[pltpu.VMEM((1024, LANES), f32), pltpu.SemaphoreType.DMA],
        compiler_params=limit,
        cost_estimate=lasting(2),
        name="emit",
    )(meta, params)
    plane_face, near, far = lax.optimization_barrier((plane_face, *got_slots[1:]))
    got_slots = [got_slots[0], near, far] + relay([near, far])

    reflux = pl.pallas_call(
        moment_kernel,
        out_shape=out((BLK * 6 * 4, LANES)),
        in_specs=[SMEM_SPEC] * 2 + [VMEM_SPEC] * 8,
        out_specs=VMEM_SPEC,
        scratch_shapes=[pltpu.VMEM((PARTS * 12, 8, LANES), f32)],
        compiler_params=limit,
        name="moments",
    )(meta, todo, plane_face, speed, slots, *got_slots)

    planes = planes.reshape(BLK, 32, 4, LANES).transpose(0, 2, 1, 3).reshape(BLK, 4, 4096)
    reflux = reflux.reshape(BLK, 6, 2, 2, LANES).transpose(0, 1, 3, 2, 4).reshape(BLK, 6, 2, 256)
    return planes, reflux


def solution(mesh):
    return jax.shard_map(
        per_device,
        mesh=mesh,
        in_specs=(
            P("sfc", None),
            P("sfc", None, None),
            P("sfc", None, None),
            P("sfc", None),
            P("sfc", None),
        ),
        out_specs=(P("sfc", None, None), P("sfc", None, None, None)),
        check_vma=False,
    )
```

time: 48.3 us -> 45.8 us (0.948); the launches traced: 47.5 us -> 45.5 us
  waiting for transfers between devices: 7.21 us -> 3 us
  Pallas kernels: 19.5 us -> 22.8 us
  starting transfers between devices: 18.4 us -> 17.4 us
    ppermute x10, waiting for transfers between devices: 7.21 us -> 3 us  [the longest x4 2.26 us: relay(): return [lax.ppermute(value, 'sfc', inside) for value in values]]
    pallas_call x2 -> x4, Pallas kernels: 17.7 us -> 20.7 us  [the longest x1 13.6 us: per_device(): pl.pallas_call(fit_kernel, out_shape=(out((4, 256, LANES)), out((12, 8, L...]
    ppermute x10, starting transfers between devices: 18.4 us -> 17.4 us  [the longest x2 12.5 us: trade(): far = lax.ppermute(value, 'sfc', partners(n, 2, 2))]
    unnamed x11 -> x3, local copies, waits for them, and re-layouts: 1.02 us -> 1 us
  transfers between devices with their start and end apart: 10 -> 10, of which waited for: 4 -> 5; matrix products, arithmetic and copies ran while one was open for 1% -> 1% of each run, Pallas kernels for 0% -> 12%
where the time goes in v2:
time: 45.8 us; the launch traced here: 45.5 us
  Pallas kernels  22.8 us (50%)
  starting transfers between devices  17.4 us (38%)
  waiting for transfers between devices  3 us (7%)
  local copies, waits for them, and re-layouts  1.33 us (3%)
  between operations  0.73 us (2%)
    pallas_call x1, Pallas kernels, per_device(): pl.pallas_call(fit_kernel, out_shape=(out((4, 256, LANES)), out((12, 8, L...  13.6 us
    ppermute x2, starting transfers between devices, trade(): far = lax.ppermute(value, 'sfc', partners(n, 2, 2))  12.5 us
    ppermute x4, starting transfers between devices, relay(): return [lax.ppermute(value, 'sfc', inside) for value in values]  3.39 us
    pallas_call x1, Pallas kernels, per_device(): pl.pallas_call(prepare_kernel, out_shape=(pltpu.HBM((7, 4, 256, LANES), f...  3.01 us
    ppermute x4, waiting for transfers between devices, relay(): return [lax.ppermute(value, 'sfc', inside) for value in values]  2.26 us
    pallas_call x1, Pallas kernels, per_device(): pl.pallas_call(emit_kernel, out_shape=(out((1024, LANES)), out((BLK * 4,...  2.24 us
    pallas_call x1, Pallas kernels, per_device(): pl.pallas_call(moment_kernel, out_shape=out((BLK * 6 * 4, LANES)), in_spe...  2.07 us
    pallas_call x1, Pallas kernels, per_device(): pl.pallas_call(pack_kernel, out_shape=(out((49, 8, LANES)), out((4, 256,...  1.89 us
  transfers between devices with their start and end apart: 10, of which 5 were waited for; matrix products, arithmetic and copies ran while one was open for 1% of the time, Pallas kernels for 12%

profile of v2, /device:TPU:25, one launch (start us, length us, event | category | flops | bytes accessed | tf_op | source)
XLA Modules:
  0.0 45.5 jit_solution(7428574414189192768)
XLA Ops:
  0.6 1.9 %pack.1 = (f32[49,8,128]{2,1,0:T(8,128)S(1)}, f32[4,256,128]{2,1,0:T(8,128)S(1)}, s32[4,16]{1,0:T(4,128)S(1)}, s32[8,6]{1,0:T(8,128)S(1)}) custom-call(f32[256,128]{1,0:T(8,128)} %bitcast.54, f32[3,256,128]{2,1,0:T(8,128)} %bitcast.53, s32[4,16]{1,0:T(4,128)} %bitcast.56, s32[8,6]{1,0:T(8,128)} %near_hbm.1), custom_call_target="tpu_custom_call" | custom-call | tf_op jit(solution)/shard_map/pack/pallas_call | solution.py:557
  2.5 8.0 %collective-permute-start.2 = (f32[49,8,128]{2,1,0:T(8,128)S(1)}, f32[49,8,128]{2,1,0:T(8,128)S(1)}, u32[]{:S(2)}, u32[]{:S(2)}) collective-permute-start(f32[49,8,128]{2,1,0:T(8,128)S(1)} %get-tuple-element.17.own_ref), channel_id=1, source_target_pairs={{0,1},{1,0},{2,4},{3,5},{4,2},{5,3},{6,8},{7,9},{8,6},{9,7},{10,12... | collective-permute-start | bytes 602120 | tf_op jit(solution)/shard_map/ppermute | solution.py:526
  10.6 0.0 collective-permute-start.1
  10.6 1.0 %collective-permute-start = (f32[49,8,128]{2,1,0:T(8,128)S(1)}, f32[49,8,128]{2,1,0:T(8,128)S(1)}, u32[]{:S(2)}, u32[]{:S(2)}) collective-permute-start(f32[49,8,128]{2,1,0:T(8,128)S(1)} %get-tuple-element.17.own_ref), channel_id=1, source_target_pairs={{0,1},{1,0},{2,3},{3,2},{4,5},{5,4},{6,7},{7,6},{8,9},{9,8},{10,11... | collective-permute-start | bytes 602120 | tf_op jit(solution)/shard_map/ppermute | solution.py:528
  11.5 0.1 select_clamp_fusion
  11.6 0.1 reshape.171.tbl_ref
  11.7 0.1 copy.11
  11.8 0.1 reshape.172.refine_ref
  11.9 0.0 copy-start
  11.9 1.0 %copy-done = f32[8,3,4096]{2,0,1:T(8,128)S(1)} copy-done((f32[8,3,4096]{2,0,1:T(8,128)S(1)}, f32[8,3,4096]{2,0,1:T(8,128)}, u32[]{:S(2)}) %copy-start) | copy-done | bytes 393240
  12.9 3.0 %prepare.1 = (f32[7,4,256,128]{3,2,1,0:T(8,128)}, f32[8,16,128]{2,1,0:T(8,128)S(1)}) custom-call(f32[4,256,128]{2,1,0:T(8,128)S(1)} %get-tuple-element.19.field, f32[3,256,128]{2,1,0:T(8,128)S(1)} %bitcast.52), custom_call_target="tpu_custom_call" | custom-call | bytes 14000000 | tf_op jit(solution)/shard_map/prepare/pallas_call | solution.py:594
  15.9 0.0 collective-permute-done.2.r3_ref
  15.9 0.6 %collective-permute-start.4 = (f32[49,8,128]{2,1,0:T(8,128)S(1)}, f32[49,8,128]{2,1,0:T(8,128)S(1)}, u32[]{:S(2)}, u32[]{:S(2)}) collective-permute-start(f32[49,8,128]{2,1,0:T(8,128)S(1)} %collective-permute-done.2.r3_ref), channel_id=1, source_target_pairs={{0,1},{1,0},{2,3},{3,2},{4,5},{5,4},{6,7},{7,6},{8,9},{9,8},{10,11... | collective-permute-start | bytes 602120 | tf_op jit(solution)/shard_map/ppermute | solution.py:533
  16.5 1.5 %collective-permute-start.3 = (f32[49,8,128]{2,1,0:T(8,128)S(1)}, f32[49,8,128]{2,1,0:T(8,128)S(1)}, u32[]{:S(2)}, u32[]{:S(2)}) collective-permute-start(f32[49,8,128]{2,1,0:T(8,128)S(1)} %collective-permute-done.1.r2_ref), channel_id=1, source_target_pairs={{0,1},{1,0},{2,3},{3,2},{4,5},{5,4},{6,7},{7,6},{8,9},{9,8},{10,11... | collective-permute-start | bytes 602120 | tf_op jit(solution)/shard_map/ppermute | solution.py:533
  18.0 0.0 collective-permute-done.r1_ref
  18.0 0.0 collective-permute-done.4.r5_ref
  18.0 1.0 %collective-permute-done.3.r4_ref = f32[49,8,128]{2,1,0:T(8,128)S(1)} collective-permute-done((f32[49,8,128]{2,1,0:T(8,128)S(1)}, f32[49,8,128]{2,1,0:T(8,128)S(1)}, u32[]{:S(2)}, u32[]{:S(2)}) %collective-permute-start.3) | collective-permute-done | bytes 200736 | tf_op jit(solution)/shard_map/ppermute | solution.py:533
  19.0 13.6 %fit.1 = (f32[4,256,128]{2,1,0:T(8,128)S(1)}, f32[12,8,128]{2,1,0:T(8,128)S(1)}) custom-call(s32[48]{0:T(128)S(1)} %reshape.171.tbl_ref, s32[32]{0:T(128)S(1)} %reshape.172.refine_ref, f32[49,8,128]{2,1,0:T(8,128)S(1)} %get-tuple-element.17.own_ref, f32[49,8,128]{2,1,0:T(8,128)S(1)} %collective-permute-done.r1_ref, ...), custom_call_target="tpu_custom_call" | custom-call | bytes 42000000 | tf_op jit(solution)/shard_map/fit/pallas_call | solution.py:609
  32.6 0.5 %collective-permute-start.7 = (f32[12,8,128]{2,1,0:T(8,128)S(1)}, f32[12,8,128]{2,1,0:T(8,128)S(1)}, u32[]{:S(2)}, u32[]{:S(2)}) collective-permute-start(f32[12,8,128]{2,1,0:T(8,128)S(1)} %get-tuple-element.26.s0_ref), channel_id=1, source_target_pairs={{0,1},{1,0},{2,3},{3,2},{4,5},{5,4},{6,7},{7,6},{8,9},{9,8},{10,11... | collective-permute-start | bytes 147464 | tf_op jit(solution)/shard_map/ppermute | solution.py:528
  33.1 4.5 %collective-permute-start.6 = (f32[12,8,128]{2,1,0:T(8,128)S(1)}, f32[12,8,128]{2,1,0:T(8,128)S(1)}, u32[]{:S(2)}, u32[]{:S(2)}) collective-permute-start(f32[12,8,128]{2,1,0:T(8,128)S(1)} %get-tuple-element.26.s0_ref), channel_id=1, source_target_pairs={{0,1},{1,0},{2,4},{3,5},{4,2},{5,3},{6,8},{7,9},{8,6},{9,7},{10,12... | collective-permute-start | bytes 147464 | tf_op jit(solution)/shard_map/ppermute | solution.py:526
  37.6 0.0 collective-permute-start.5
  37.6 0.1 and_convert_fusion
  37.8 0.1 reshape.170.meta_ref
  37.8 2.2 %emit.1 = (f32[1024,128]{1,0:T(8,128)}, f32[32,16,128]{2,1,0:T(8,128)S(1)}, s32[112]{0:T(128)S(1)}) custom-call(s32[384]{0:T(512)S(1)} %reshape.170.meta_ref, f32[4,256,128]{2,1,0:T(8,128)S(1)} %get-tuple-element.22.params), custom_call_target="tpu_custom_call" | custom-call | bytes 7000000 | tf_op jit(solution)/shard_map/emit/pallas_call | solution.py:643
  40.1 0.1 collective-permute-done.6.s3_ref
  40.2 0.6 %collective-permute-done.5.s2_ref = f32[12,8,128]{2,1,0:T(8,128)S(1)} collective-permute-done((f32[12,8,128]{2,1,0:T(8,128)S(1)}, f32[12,8,128]{2,1,0:T(8,128)S(1)}, u32[]{:S(2)}, u32[]{:S(2)}) %collective-permute-start.5) | collective-permute-done | bytes 49184 | tf_op jit(solution)/shard_map/ppermute | solution.py:527
  40.8 1.4 %collective-permute-start.8 = (f32[12,8,128]{2,1,0:T(8,128)S(1)}, f32[12,8,128]{2,1,0:T(8,128)S(1)}, u32[]{:S(2)}, u32[]{:S(2)}) collective-permute-start(f32[12,8,128]{2,1,0:T(8,128)S(1)} %collective-permute-done.5.s2_ref), channel_id=1, source_target_pairs={{0,1},{1,0},{2,3},{3,2},{4,5},{5,4},{6,7},{7,6},{8,9},{9,8},{10,11... | collective-permute-start | bytes 147464 | tf_op jit(solution)/shard_map/ppermute | solution.py:533
  42.2 0.0 collective-permute-start.9
  42.2 0.0 collective-permute-done.7.s1_ref
  42.2 0.9 %collective-permute-done.8.s4_ref = f32[12,8,128]{2,1,0:T(8,128)S(1)} collective-permute-done((f32[12,8,128]{2,1,0:T(8,128)S(1)}, f32[12,8,128]{2,1,0:T(8,128)S(1)}, u32[]{:S(2)}, u32[]{:S(2)}) %collective-permute-start.8) | collective-permute-done | bytes 49184 | tf_op jit(solution)/shard_map/ppermute | solution.py:533
  43.1 0.3 collective-permute-done.9.s5_ref
  43.4 2.1 %moments.1 = f32[192,128]{1,0:T(8,128)} custom-call(s32[384]{0:T(512)S(1)} %reshape.170.meta_ref, s32[112]{0:T(128)S(1)} %get-tuple-element.24.todo, f32[32,16,128]{2,1,0:T(8,128)S(1)} %get-tuple-element.27.pf_ref, f32[8,16,128]{2,1,0:T(8,128)S(1)} %get-tuple-element.21.speed_ref, f32[12,8,128]{2,1,0:T(8,128)S(1)} %get-tuple-element.26.s0_ref, ...), custom_call_target="tpu_custom_call" | custom-call | tf_op jit(solution)/shard_map/moments/pallas_call | solution.py:660
  (15 shorter events, 0.1 us)
Async XLA Ops:
  2.5 13.4 %collective-permute-start.2 = (f32[49,8,128]{2,1,0:T(8,128)S(1)}, f32[49,8,128]{2,1,0:T(8,128)S(1)}, u32[]{:S(2)}, u32[]{:S(2)}) collective-permute-start(f32[49,8,128]{2,1,0:T(8,128)S(1)} %get-tuple-element.17.own_ref), channel_id=1, source_target_pairs={{0,1},{1,0},{2,4},{3,5},{4,2},{5,3},{6,8},{7,9},{8,6},{9,7},{10,12... | collective-permute-start | bytes 602120 | tf_op jit(solution)/shard_map/ppermute | solution.py:526
  10.6 5.9 %collective-permute-start.1 = (f32[49,8,128]{2,1,0:T(8,128)S(1)}, f32[49,8,128]{2,1,0:T(8,128)S(1)}, u32[]{:S(2)}, u32[]{:S(2)}) collective-permute-start(f32[49,8,128]{2,1,0:T(8,128)S(1)} %get-tuple-element.17.own_ref), channel_id=1, source_target_pairs={{0,2},{1,3},{2,0},{3,1},{4,6},{5,7},{6,4},{7,5},{8,10},{9,11},{10,... | collective-permute-start | bytes 602120 | tf_op jit(solution)/shard_map/ppermute | solution.py:527
  10.6 7.4 %collective-permute-start = (f32[49,8,128]{2,1,0:T(8,128)S(1)}, f32[49,8,128]{2,1,0:T(8,128)S(1)}, u32[]{:S(2)}, u32[]{:S(2)}) collective-permute-start(f32[49,8,128]{2,1,0:T(8,128)S(1)} %get-tuple-element.17.own_ref), channel_id=1, source_target_pairs={{0,1},{1,0},{2,3},{3,2},{4,5},{5,4},{6,7},{7,6},{8,9},{9,8},{10,11... | collective-permute-start | bytes 602120 | tf_op jit(solution)/shard_map/ppermute | solution.py:528
  11.9 1.0 %copy-start = (f32[8,3,4096]{2,0,1:T(8,128)S(1)}, f32[8,3,4096]{2,0,1:T(8,128)}, u32[]{:S(2)}) copy-start(f32[8,3,4096]{2,0,1:T(8,128)} %param.7) | copy-start | bytes 1179652
  15.9 2.1 %collective-permute-start.4 = (f32[49,8,128]{2,1,0:T(8,128)S(1)}, f32[49,8,128]{2,1,0:T(8,128)S(1)}, u32[]{:S(2)}, u32[]{:S(2)}) collective-permute-start(f32[49,8,128]{2,1,0:T(8,128)S(1)} %collective-permute-done.2.r3_ref), channel_id=1, source_target_pairs={{0,1},{1,0},{2,3},{3,2},{4,5},{5,4},{6,7},{7,6},{8,9},{9,8},{10,11... | collective-permute-start | bytes 602120 | tf_op jit(solution)/shard_map/ppermute | solution.py:533
  16.5 2.5 %collective-permute-start.3 = (f32[49,8,128]{2,1,0:T(8,128)S(1)}, f32[49,8,128]{2,1,0:T(8,128)S(1)}, u32[]{:S(2)}, u32[]{:S(2)}) collective-permute-start(f32[49,8,128]{2,1,0:T(8,128)S(1)} %collective-permute-done.1.r2_ref), channel_id=1, source_target_pairs={{0,1},{1,0},{2,3},{3,2},{4,5},{5,4},{6,7},{7,6},{8,9},{9,8},{10,11... | collective-permute-start | bytes 602120 | tf_op jit(solution)/shard_map/ppermute | solution.py:533
  32.6 9.6 %collective-permute-start.7 = (f32[12,8,128]{2,1,0:T(8,128)S(1)}, f32[12,8,128]{2,1,0:T(8,128)S(1)}, u32[]{:S(2)}, u32[]{:S(2)}) collective-permute-start(f32[12,8,128]{2,1,0:T(8,128)S(1)} %get-tuple-element.26.s0_ref), channel_id=1, source_target_pairs={{0,1},{1,0},{2,3},{3,2},{4,5},{5,4},{6,7},{7,6},{8,9},{9,8},{10,11... | collective-permute-start | bytes 147464 | tf_op jit(solution)/shard_map/ppermute | solution.py:528
  33.1 7.2 %collective-permute-start.6 = (f32[12,8,128]{2,1,0:T(8,128)S(1)}, f32[12,8,128]{2,1,0:T(8,128)S(1)}, u32[]{:S(2)}, u32[]{:S(2)}) collective-permute-start(f32[12,8,128]{2,1,0:T(8,128)S(1)} %get-tuple-element.26.s0_ref), channel_id=1, source_target_pairs={{0,1},{1,0},{2,4},{3,5},{4,2},{5,3},{6,8},{7,9},{8,6},{9,7},{10,12... | collective-permute-start | bytes 147464 | tf_op jit(solution)/shard_map/ppermute | solution.py:526
  37.6 3.2 %collective-permute-start.5 = (f32[12,8,128]{2,1,0:T(8,128)S(1)}, f32[12,8,128]{2,1,0:T(8,128)S(1)}, u32[]{:S(2)}, u32[]{:S(2)}) collective-permute-start(f32[12,8,128]{2,1,0:T(8,128)S(1)} %get-tuple-element.26.s0_ref), channel_id=1, source_target_pairs={{0,2},{1,3},{2,0},{3,1},{4,6},{5,7},{6,4},{7,5},{8,10},{9,11},{10,... | collective-permute-start | bytes 147464 | tf_op jit(solution)/shard_map/ppermute | solution.py:527
  40.8 2.2 %collective-permute-start.8 = (f32[12,8,128]{2,1,0:T(8,128)S(1)}, f32[12,8,128]{2,1,0:T(8,128)S(1)}, u32[]{:S(2)}, u32[]{:S(2)}) collective-permute-start(f32[12,8,128]{2,1,0:T(8,128)S(1)} %collective-permute-done.5.s2_ref), channel_id=1, source_target_pairs={{0,1},{1,0},{2,3},{3,2},{4,5},{5,4},{6,7},{7,6},{8,9},{9,8},{10,11... | collective-permute-start | bytes 147464 | tf_op jit(solution)/shard_map/ppermute | solution.py:533
  42.2 1.2 %collective-permute-start.9 = (f32[12,8,128]{2,1,0:T(8,128)S(1)}, f32[12,8,128]{2,1,0:T(8,128)S(1)}, u32[]{:S(2)}, u32[]{:S(2)}) collective-permute-start(f32[12,8,128]{2,1,0:T(8,128)S(1)} %collective-permute-done.6.s3_ref), channel_id=1, source_target_pairs={{0,1},{1,0},{2,3},{3,2},{4,5},{5,4},{6,7},{7,6},{8,9},{9,8},{10,11... | collective-permute-start | bytes 147464 | tf_op jit(solution)/shard_map/ppermute | solution.py:533

commit v3 on v2

--- a/solution.py
+++ b/solution.py
@@ -57,24 +57,26 @@
     lane = lane_ids()
     index, upper = side_index(lane)
     out_ref[48] = jnp.zeros((8, LANES), jnp.float32)
-    for copy in copies:
+    for fp in (0, 1):
+
+        def block(b, carry, fp=fp):
+            for xh in (0, 1):
+                sides = []
+                for f in (2 * fp, 2 * fp + 1):
+                    half = [cells(field.at[f], b, xh, yh) for yh in (0, 1)]
+                    for yh in (0, 1):
+                        row = half[yh][0:1] if xh == 0 else half[yh][7:8]
+                        out_ref[b * 6 + xh, 2 * f + yh : 2 * f + yh + 1, :] = row
+                    sides.append(jnp.where(upper, pick(half[1], index), pick(half[0], index)))
+                out_ref[b * 6 + 2 + 2 * fp + xh] = jnp.where(lane < 64, sides[0], sides[1])
+            return carry
+
+        copies[2 * fp].wait()
+        copies[2 * fp + 1].wait()
+        lax.fori_loop(0, BLK, block, 0, unroll=4)
+    for copy in copies[4:]:
         copy.wait()
     out_ref[48, 0:4, 0:SLOTS] = refine_ref[...].astype(jnp.float32)
-
-    def block(b, carry):
-        for xh in (0, 1):
-            sides = []
-            for f in range(4):
-                half = [cells(field.at[f], b, xh, yh) for yh in (0, 1)]
-                for yh in (0, 1):
-                    row = half[yh][0:1] if xh == 0 else half[yh][7:8]
-                    out_ref[b * 6 + xh, 2 * f + yh : 2 * f + yh + 1, :] = row
-                sides.append(jnp.where(upper, pick(half[1], index), pick(half[0], index)))
-            for fp in (0, 1):
-                out_ref[b * 6 + 2 + 2 * fp + xh] = jnp.where(lane < 64, sides[2 * fp], sides[2 * fp + 1])
-        return carry
-
-    lax.fori_loop(0, BLK, block, 0)
 
 
 def solve(h, g):
@@ -350,7 +352,7 @@
             slots_ref[4 * comp + g] = total[comp]
         return carry
 
-    lax.fori_loop(0, SLOTS // 4, tile, 0)
+    lax.fori_loop(0, SLOTS // 4, tile, 0, unroll=2)
 
 
 def fit_kernel(
@@ -363,8 +365,8 @@
         )
         for b in range(BLK)
     ]
-    for fetch in fetches:
-        fetch.start()
+    fetches[0].start()
+    fetches[1].start()
     lane = lane_ids()
     for at, ref in enumerate((own_ref, r1_ref, r2_ref, r3_ref, r4_ref, r5_ref)):
 
@@ -387,13 +389,15 @@
     lax.fori_loop(0, BLK, swap, 0, unroll=2)
     for b in range(BLK):
         fetches[b].wait()
+        if b + 2 < BLK:
+            fetches[b + 2].start()
         patch(b, tbl_ref, table, st)
         at = slice(b * 32, b * 32 + 32)
 
         def load(j, at=at):
             return tuple(st[j, c, at, :] for c in range(4))
 
-        values = lax.fori_loop(0, PASSES, lambda _, p, load=load: one_pass(load, p), start(load))
+        values = lax.fori_loop(0, PASSES, lambda _, p, load=load: one_pass(load, p), start(load), unroll=6)
         for comp in range(4):
             params[comp, at, :] = values[comp]
     fine_slots(refine_ref, params, speed_ref, slots_ref)
@@ -415,7 +419,7 @@
     plane_faces(params, pf_ref, BLK, 0)
 
     def collect(i, n):
-        todo_ref[n] = i
+        todo_ref[n] = meta_ref[PARTS * SLOTS + i]
         return n + meta_ref[i]
 
     count = lax.fori_loop(0, PARTS * SLOTS, collect, 0, unroll=8)
@@ -426,7 +430,7 @@
 
 
 def moment_kernel(
-    meta_ref, todo, pf_ref, speed_ref, s0_ref, s1_ref, s2_ref, s3_ref, s4_ref, s5_ref, out_ref, slots
+    todo, pf_ref, speed_ref, s0_ref, s1_ref, s2_ref, s3_ref, s4_ref, s5_ref, out_ref, slots
 ):
     lane = lane_ids()
     row = row_ids()
@@ -434,7 +438,6 @@
     for at, ref in enumerate((s0_ref, s1_ref, s2_ref, s3_ref, s4_ref, s5_ref)):
         for u in range(12):
             slots[at * 12 + u] = ref[u]
-    total = PARTS * SLOTS
 
     count = todo[TODO - 1]
     quarter = lane // 32
@@ -453,10 +456,11 @@
 
         for q in range(4):
             at = 4 * g + q
-            i = todo[at]
-            c = meta_ref[total + i]
-            k = meta_ref[2 * total + i]
-            quad = meta_ref[3 * total + i]
+            entry = todo[at]
+            i = entry & 127
+            c = lax.shift_right_logical(entry, 7) & 7
+            k = lax.shift_right_logical(entry, 10) & 7
+            quad = lax.shift_right_logical(entry, 13)
             axis = lax.shift_right_logical(k, 1)
             qa = lax.shift_right_logical(quad, 1)
             qb = quad & 1
@@ -631,14 +635,14 @@
     fresh = jnp.logical_not(twice & ((part_ids == 3) | (part_ids == 5)))
     mine = (tables[0] >= 0) & (tables[2] // BLK == me) & fresh
     side = jnp.clip(tables[1], 0, 5)
-    meta = jnp.stack(
-        [
-            mine.astype(i32),
-            jnp.clip(tables[2], 0, None) % BLK,
-            side + 1 - 2 * (side % 2),
-            jnp.clip(tables[3], 0, 3),
-        ]
-    ).reshape(4 * PARTS * SLOTS)
+    slot_ids = jnp.arange(PARTS * SLOTS, dtype=i32).reshape(PARTS, SLOTS)
+    entry = (
+        slot_ids
+        + 128 * (jnp.clip(tables[2], 0, None) % BLK)
+        + 1024 * (side + 1 - 2 * (side % 2))
+        + 8192 * jnp.clip(tables[3], 0, 3)
+    )
+    meta = jnp.stack([mine.astype(i32), entry]).reshape(2 * PARTS * SLOTS)
 
     planes, plane_face, todo = pl.pallas_call(
         emit_kernel,
@@ -660,12 +664,12 @@
     reflux = pl.pallas_call(
         moment_kernel,
         out_shape=out((BLK * 6 * 4, LANES)),
-        in_specs=[SMEM_SPEC] * 2 + [VMEM_SPEC] * 8,
+        in_specs=[SMEM_SPEC] + [VMEM_SPEC] * 8,
         out_specs=VMEM_SPEC,
         scratch_shapes=[pltpu.VMEM((PARTS * 12, 8, LANES), f32)],
         compiler_params=limit,
         name="moments",
-    )(meta, todo, plane_face, speed, slots, *got_slots)
+    )(todo, plane_face, speed, slots, *got_slots)
 
     planes = planes.reshape(BLK, 32, 4, LANES).transpose(0, 2, 1, 3).reshape(BLK, 4, 4096)
     reflux = reflux.reshape(BLK, 6, 2, 2, LANES).transpose(0, 1, 3, 2, 4).reshape(BLK, 6, 2, 256)

time: 45.8 us -> 44.8 us (0.978)
  Pallas kernels: 22.8 us -> 21.7 us
    pallas_call x1, Pallas kernels: 13.6 us -> 12.8 us  [per_device(): pl.pallas_call(fit_kernel, out_shape=(out((4, 256, LANES)), out((12, 8, L...]
where the time goes in v3:
time: 44.8 us; the launch traced here: 44.3 us
  Pallas kernels  21.7 us (48%)
  starting transfers between devices  17.3 us (39%)
  waiting for transfers between devices  2.97 us (7%)
  local copies, waits for them, and re-layouts  1.33 us (3%)
  between operations  0.73 us (2%)
    pallas_call x1, Pallas kernels, per_device(): pl.pallas_call(fit_kernel, out_shape=(out((4, 256, LANES)), out((12, 8, L...  12.8 us
    ppermute x2, starting transfers between devices, trade(): far = lax.ppermute(value, 'sfc', partners(n, 2, 2))  12.5 us
    ppermute x4, starting transfers between devices, relay(): return [lax.ppermute(value, 'sfc', inside) for value in values]  3.38 us
    pallas_call x1, Pallas kernels, per_device(): pl.pallas_call(prepare_kernel, out_shape=(pltpu.HBM((7, 4, 256, LANES), f...  3.01 us
    pallas_call x1, Pallas kernels, per_device(): pl.pallas_call(emit_kernel, out_shape=(out((1024, LANES)), out((BLK * 4,...  2.28 us
    ppermute x4, waiting for transfers between devices, relay(): return [lax.ppermute(value, 'sfc', inside) for value in values]  2.26 us
    pallas_call x1, Pallas kernels, per_device(): pl.pallas_call(moment_kernel, out_shape=out((BLK * 6 * 4, LANES)), in_spe...  2.05 us
    pallas_call x1, Pallas kernels, per_device(): pl.pallas_call(pack_kernel, out_shape=(out((49, 8, LANES)), out((4, 256,...  1.48 us
  transfers between devices with their start and end apart: 10, of which 5 were waited for; matrix products, arithmetic and copies ran while one was open for 1% of the time, Pallas kernels for 12%

profile of v3, /device:TPU:25, one launch (start us, length us, event | category | flops | bytes accessed | tf_op | source)
XLA Modules:
  0.0 44.3 jit_solution(6727730056083996767)
XLA Ops:
  0.6 1.5 %pack.1 = (f32[49,8,128]{2,1,0:T(8,128)S(1)}, f32[4,256,128]{2,1,0:T(8,128)S(1)}, s32[4,16]{1,0:T(4,128)S(1)}, s32[8,6]{1,0:T(8,128)S(1)}) custom-call(f32[256,128]{1,0:T(8,128)} %bitcast.54, f32[3,256,128]{2,1,0:T(8,128)} %bitcast.53, s32[4,16]{1,0:T(4,128)} %bitcast.56, s32[8,6]{1,0:T(8,128)} %near_hbm.1), custom_call_target="tpu_custom_call" | custom-call | tf_op jit(solution)/shard_map/pack/pallas_call | solution.py:561
  2.1 8.0 %collective-permute-start.2 = (f32[49,8,128]{2,1,0:T(8,128)S(1)}, f32[49,8,128]{2,1,0:T(8,128)S(1)}, u32[]{:S(2)}, u32[]{:S(2)}) collective-permute-start(f32[49,8,128]{2,1,0:T(8,128)S(1)} %get-tuple-element.17.own_ref), channel_id=1, source_target_pairs={{0,1},{1,0},{2,4},{3,5},{4,2},{5,3},{6,8},{7,9},{8,6},{9,7},{10,12... | collective-permute-start | bytes 602120 | tf_op jit(solution)/shard_map/ppermute | solution.py:530
  10.2 0.0 collective-permute-start.1
  10.2 1.0 %collective-permute-start = (f32[49,8,128]{2,1,0:T(8,128)S(1)}, f32[49,8,128]{2,1,0:T(8,128)S(1)}, u32[]{:S(2)}, u32[]{:S(2)}) collective-permute-start(f32[49,8,128]{2,1,0:T(8,128)S(1)} %get-tuple-element.17.own_ref), channel_id=1, source_target_pairs={{0,1},{1,0},{2,3},{3,2},{4,5},{5,4},{6,7},{7,6},{8,9},{9,8},{10,11... | collective-permute-start | bytes 602120 | tf_op jit(solution)/shard_map/ppermute | solution.py:532
  11.1 0.1 select_clamp_fusion
  11.2 0.1 reshape.195.tbl_ref
  11.3 0.1 copy.11
  11.4 0.1 reshape.196.refine_ref
  11.5 0.0 copy-start
  11.5 1.0 %copy-done = f32[8,3,4096]{2,0,1:T(8,128)S(1)} copy-done((f32[8,3,4096]{2,0,1:T(8,128)S(1)}, f32[8,3,4096]{2,0,1:T(8,128)}, u32[]{:S(2)}) %copy-start) | copy-done | bytes 393240
  12.5 3.0 %prepare.1 = (f32[7,4,256,128]{3,2,1,0:T(8,128)}, f32[8,16,128]{2,1,0:T(8,128)S(1)}) custom-call(f32[4,256,128]{2,1,0:T(8,128)S(1)} %get-tuple-element.19.field, f32[3,256,128]{2,1,0:T(8,128)S(1)} %bitcast.52), custom_call_target="tpu_custom_call" | custom-call | bytes 14000000 | tf_op jit(solution)/shard_map/prepare/pallas_call | solution.py:598
  15.5 0.0 collective-permute-done.2.r3_ref
  15.5 0.6 %collective-permute-start.4 = (f32[49,8,128]{2,1,0:T(8,128)S(1)}, f32[49,8,128]{2,1,0:T(8,128)S(1)}, u32[]{:S(2)}, u32[]{:S(2)}) collective-permute-start(f32[49,8,128]{2,1,0:T(8,128)S(1)} %collective-permute-done.2.r3_ref), channel_id=1, source_target_pairs={{0,1},{1,0},{2,3},{3,2},{4,5},{5,4},{6,7},{7,6},{8,9},{9,8},{10,11... | collective-permute-start | bytes 602120 | tf_op jit(solution)/shard_map/ppermute | solution.py:537
  16.1 0.0 collective-permute-done.1.r2_ref
  16.1 1.5 %collective-permute-start.3 = (f32[49,8,128]{2,1,0:T(8,128)S(1)}, f32[49,8,128]{2,1,0:T(8,128)S(1)}, u32[]{:S(2)}, u32[]{:S(2)}) collective-permute-start(f32[49,8,128]{2,1,0:T(8,128)S(1)} %collective-permute-done.1.r2_ref), channel_id=1, source_target_pairs={{0,1},{1,0},{2,3},{3,2},{4,5},{5,4},{6,7},{7,6},{8,9},{9,8},{10,11... | collective-permute-start | bytes 602120 | tf_op jit(solution)/shard_map/ppermute | solution.py:537
  17.6 0.0 collective-permute-done.r1_ref
  17.6 0.0 collective-permute-done.4.r5_ref
  17.6 1.0 %collective-permute-done.3.r4_ref = f32[49,8,128]{2,1,0:T(8,128)S(1)} collective-permute-done((f32[49,8,128]{2,1,0:T(8,128)S(1)}, f32[49,8,128]{2,1,0:T(8,128)S(1)}, u32[]{:S(2)}, u32[]{:S(2)}) %collective-permute-start.3) | collective-permute-done | bytes 200736 | tf_op jit(solution)/shard_map/ppermute | solution.py:537
  18.6 12.8 %fit.1 = (f32[4,256,128]{2,1,0:T(8,128)S(1)}, f32[12,8,128]{2,1,0:T(8,128)S(1)}) custom-call(s32[48]{0:T(128)S(1)} %reshape.195.tbl_ref, s32[32]{0:T(128)S(1)} %reshape.196.refine_ref, f32[49,8,128]{2,1,0:T(8,128)S(1)} %get-tuple-element.17.own_ref, f32[49,8,128]{2,1,0:T(8,128)S(1)} %collective-permute-done.r1_ref, ...), custom_call_target="tpu_custom_call" | custom-call | bytes 42000000 | tf_op jit(solution)/shard_map/fit/pallas_call | solution.py:613
  31.5 0.5 %collective-permute-start.7 = (f32[12,8,128]{2,1,0:T(8,128)S(1)}, f32[12,8,128]{2,1,0:T(8,128)S(1)}, u32[]{:S(2)}, u32[]{:S(2)}) collective-permute-start(f32[12,8,128]{2,1,0:T(8,128)S(1)} %get-tuple-element.26.s0_ref), channel_id=1, source_target_pairs={{0,1},{1,0},{2,3},{3,2},{4,5},{5,4},{6,7},{7,6},{8,9},{9,8},{10,11... | collective-permute-start | bytes 147464 | tf_op jit(solution)/shard_map/ppermute | solution.py:532
  31.9 4.5 %collective-permute-start.6 = (f32[12,8,128]{2,1,0:T(8,128)S(1)}, f32[12,8,128]{2,1,0:T(8,128)S(1)}, u32[]{:S(2)}, u32[]{:S(2)}) collective-permute-start(f32[12,8,128]{2,1,0:T(8,128)S(1)} %get-tuple-element.26.s0_ref), channel_id=1, source_target_pairs={{0,1},{1,0},{2,4},{3,5},{4,2},{5,3},{6,8},{7,9},{8,6},{9,7},{10,12... | collective-permute-start | bytes 147464 | tf_op jit(solution)/shard_map/ppermute | solution.py:530
  36.5 0.1 and_convert_fusion
  36.6 0.1 reshape.194.meta_ref
  36.7 2.3 %emit.1 = (f32[1024,128]{1,0:T(8,128)}, f32[32,16,128]{2,1,0:T(8,128)S(1)}, s32[112]{0:T(128)S(1)}) custom-call(s32[192]{0:T(256)S(1)} %reshape.194.meta_ref, f32[4,256,128]{2,1,0:T(8,128)S(1)} %get-tuple-element.22.params), custom_call_target="tpu_custom_call" | custom-call | bytes 7000000 | tf_op jit(solution)/shard_map/emit/pallas_call | solution.py:647
  39.0 0.1 collective-permute-done.6.s3_ref
  39.1 0.6 %collective-permute-done.5.s2_ref = f32[12,8,128]{2,1,0:T(8,128)S(1)} collective-permute-done((f32[12,8,128]{2,1,0:T(8,128)S(1)}, f32[12,8,128]{2,1,0:T(8,128)S(1)}, u32[]{:S(2)}, u32[]{:S(2)}) %collective-permute-start.5) | collective-permute-done | bytes 49184 | tf_op jit(solution)/shard_map/ppermute | solution.py:531
  39.7 1.4 %collective-permute-start.8 = (f32[12,8,128]{2,1,0:T(8,128)S(1)}, f32[12,8,128]{2,1,0:T(8,128)S(1)}, u32[]{:S(2)}, u32[]{:S(2)}) collective-permute-start(f32[12,8,128]{2,1,0:T(8,128)S(1)} %collective-permute-done.5.s2_ref), channel_id=1, source_target_pairs={{0,1},{1,0},{2,3},{3,2},{4,5},{5,4},{6,7},{7,6},{8,9},{9,8},{10,11... | collective-permute-start | bytes 147464 | tf_op jit(solution)/shard_map/ppermute | solution.py:537
  41.0 0.0 collective-permute-start.9
  41.1 0.0 collective-permute-done.7.s1_ref
  41.1 0.9 %collective-permute-done.8.s4_ref = f32[12,8,128]{2,1,0:T(8,128)S(1)} collective-permute-done((f32[12,8,128]{2,1,0:T(8,128)S(1)}, f32[12,8,128]{2,1,0:T(8,128)S(1)}, u32[]{:S(2)}, u32[]{:S(2)}) %collective-permute-start.8) | collective-permute-done | bytes 49184 | tf_op jit(solution)/shard_map/ppermute | solution.py:537
  41.9 0.3 collective-permute-done.9.s5_ref
  42.3 2.0 %moments.1 = f32[192,128]{1,0:T(8,128)} custom-call(s32[112]{0:T(128)S(1)} %get-tuple-element.24.todo, f32[32,16,128]{2,1,0:T(8,128)S(1)} %get-tuple-element.27.pf_ref, f32[8,16,128]{2,1,0:T(8,128)S(1)} %get-tuple-element.21.speed_ref, f32[12,8,128]{2,1,0:T(8,128)S(1)} %get-tuple-element.26.s0_ref, f32[12,8,128]{2,1,0:T(8,128)S(1)} %collective-permute-done.7.s1_ref, ...), custom_call_target="tpu_custom_call" | custom-call | tf_op jit(solution)/shard_map/moments/pallas_call | solution.py:664
  (15 shorter events, 0.1 us)
Async XLA Ops:
  2.1 13.4 %collective-permute-start.2 = (f32[49,8,128]{2,1,0:T(8,128)S(1)}, f32[49,8,128]{2,1,0:T(8,128)S(1)}, u32[]{:S(2)}, u32[]{:S(2)}) collective-permute-start(f32[49,8,128]{2,1,0:T(8,128)S(1)} %get-tuple-element.17.own_ref), channel_id=1, source_target_pairs={{0,1},{1,0},{2,4},{3,5},{4,2},{5,3},{6,8},{7,9},{8,6},{9,7},{10,12... | collective-permute-start | bytes 602120 | tf_op jit(solution)/shard_map/ppermute | solution.py:530
  10.2 5.9 %collective-permute-start.1 = (f32[49,8,128]{2,1,0:T(8,128)S(1)}, f32[49,8,128]{2,1,0:T(8,128)S(1)}, u32[]{:S(2)}, u32[]{:S(2)}) collective-permute-start(f32[49,8,128]{2,1,0:T(8,128)S(1)} %get-tuple-element.17.own_ref), channel_id=1, source_target_pairs={{0,2},{1,3},{2,0},{3,1},{4,6},{5,7},{6,4},{7,5},{8,10},{9,11},{10,... | collective-permute-start | bytes 602120 | tf_op jit(solution)/shard_map/ppermute | solution.py:531
  10.2 7.4 %collective-permute-start = (f32[49,8,128]{2,1,0:T(8,128)S(1)}, f32[49,8,128]{2,1,0:T(8,128)S(1)}, u32[]{:S(2)}, u32[]{:S(2)}) collective-permute-start(f32[49,8,128]{2,1,0:T(8,128)S(1)} %get-tuple-element.17.own_ref), channel_id=1, source_target_pairs={{0,1},{1,0},{2,3},{3,2},{4,5},{5,4},{6,7},{7,6},{8,9},{9,8},{10,11... | collective-permute-start | bytes 602120 | tf_op jit(solution)/shard_map/ppermute | solution.py:532
  11.5 1.0 %copy-start = (f32[8,3,4096]{2,0,1:T(8,128)S(1)}, f32[8,3,4096]{2,0,1:T(8,128)}, u32[]{:S(2)}) copy-start(f32[8,3,4096]{2,0,1:T(8,128)} %param.7) | copy-start | bytes 1179652
  15.5 2.1 %collective-permute-start.4 = (f32[49,8,128]{2,1,0:T(8,128)S(1)}, f32[49,8,128]{2,1,0:T(8,128)S(1)}, u32[]{:S(2)}, u32[]{:S(2)}) collective-permute-start(f32[49,8,128]{2,1,0:T(8,128)S(1)} %collective-permute-done.2.r3_ref), channel_id=1, source_target_pairs={{0,1},{1,0},{2,3},{3,2},{4,5},{5,4},{6,7},{7,6},{8,9},{9,8},{10,11... | collective-permute-start | bytes 602120 | tf_op jit(solution)/shard_map/ppermute | solution.py:537
  16.1 2.5 %collective-permute-start.3 = (f32[49,8,128]{2,1,0:T(8,128)S(1)}, f32[49,8,128]{2,1,0:T(8,128)S(1)}, u32[]{:S(2)}, u32[]{:S(2)}) collective-permute-start(f32[49,8,128]{2,1,0:T(8,128)S(1)} %collective-permute-done.1.r2_ref), channel_id=1, source_target_pairs={{0,1},{1,0},{2,3},{3,2},{4,5},{5,4},{6,7},{7,6},{8,9},{9,8},{10,11... | collective-permute-start | bytes 602120 | tf_op jit(solution)/shard_map/ppermute | solution.py:537
  31.5 9.6 %collective-permute-start.7 = (f32[12,8,128]{2,1,0:T(8,128)S(1)}, f32[12,8,128]{2,1,0:T(8,128)S(1)}, u32[]{:S(2)}, u32[]{:S(2)}) collective-permute-start(f32[12,8,128]{2,1,0:T(8,128)S(1)} %get-tuple-element.26.s0_ref), channel_id=1, source_target_pairs={{0,1},{1,0},{2,3},{3,2},{4,5},{5,4},{6,7},{7,6},{8,9},{9,8},{10,11... | collective-permute-start | bytes 147464 | tf_op jit(solution)/shard_map/ppermute | solution.py:532
  31.9 7.2 %collective-permute-start.6 = (f32[12,8,128]{2,1,0:T(8,128)S(1)}, f32[12,8,128]{2,1,0:T(8,128)S(1)}, u32[]{:S(2)}, u32[]{:S(2)}) collective-permute-start(f32[12,8,128]{2,1,0:T(8,128)S(1)} %get-tuple-element.26.s0_ref), channel_id=1, source_target_pairs={{0,1},{1,0},{2,4},{3,5},{4,2},{5,3},{6,8},{7,9},{8,6},{9,7},{10,12... | collective-permute-start | bytes 147464 | tf_op jit(solution)/shard_map/ppermute | solution.py:530
  36.4 3.2 %collective-permute-start.5 = (f32[12,8,128]{2,1,0:T(8,128)S(1)}, f32[12,8,128]{2,1,0:T(8,128)S(1)}, u32[]{:S(2)}, u32[]{:S(2)}) collective-permute-start(f32[12,8,128]{2,1,0:T(8,128)S(1)} %get-tuple-element.26.s0_ref), channel_id=1, source_target_pairs={{0,2},{1,3},{2,0},{3,1},{4,6},{5,7},{6,4},{7,5},{8,10},{9,11},{10,... | collective-permute-start | bytes 147464 | tf_op jit(solution)/shard_map/ppermute | solution.py:531
  39.7 2.2 %collective-permute-start.8 = (f32[12,8,128]{2,1,0:T(8,128)S(1)}, f32[12,8,128]{2,1,0:T(8,128)S(1)}, u32[]{:S(2)}, u32[]{:S(2)}) collective-permute-start(f32[12,8,128]{2,1,0:T(8,128)S(1)} %collective-permute-done.5.s2_ref), channel_id=1, source_target_pairs={{0,1},{1,0},{2,3},{3,2},{4,5},{5,4},{6,7},{7,6},{8,9},{9,8},{10,11... | collective-permute-start | bytes 147464 | tf_op jit(solution)/shard_map/ppermute | solution.py:537
  41.0 1.2 %collective-permute-start.9 = (f32[12,8,128]{2,1,0:T(8,128)S(1)}, f32[12,8,128]{2,1,0:T(8,128)S(1)}, u32[]{:S(2)}, u32[]{:S(2)}) collective-permute-start(f32[12,8,128]{2,1,0:T(8,128)S(1)} %collective-permute-done.6.s3_ref), channel_id=1, source_target_pairs={{0,1},{1,0},{2,3},{3,2},{4,5},{5,4},{6,7},{7,6},{8,9},{9,8},{10,11... | collective-permute-start | bytes 147464 | tf_op jit(solution)/shard_map/ppermute | solution.py:537

commit v4 on v3

--- a/solution.py
+++ b/solution.py
@@ -11,6 +11,7 @@
 SLOTS = 16
 PARTS = 6
 TODO = 112
+EARLY = 4
 PASSES = 6
 LANES = 128
 NODES = (0.5 - 3.0**0.5 / 6.0, 0.5 + 3.0**0.5 / 6.0)
@@ -240,10 +241,13 @@
     return low, high
 
 
-def prepare_kernel(field, velo_ref, points_hbm, out_ref, xpad, st, sem):
+def prepare_kernel(field, velo_hbm, points_hbm, out_ref, xpad, st, velo_ref, sem, velo_sem):
+    fetch = pltpu.make_async_copy(velo_hbm, velo_ref, velo_sem)
+    fetch.start()
     own_points(field, xpad, st)
     keep = pltpu.make_async_copy(st, points_hbm, sem)
     keep.start()
+    fetch.wait()
     lane, row = lane_ids(), row_ids()
     index, upper = face_index(lane)
 
@@ -403,7 +407,7 @@
     fine_slots(refine_ref, params, speed_ref, slots_ref)
 
 
-def emit_kernel(meta_ref, params, planes_hbm, pf_ref, todo_ref, buffer, sem):
+def emit_kernel(meta_ref, params, planes_hbm, pf_ref, early_ref, late_ref, buffer, sem):
     def emit(b, carry):
         for comp in range(4):
             for xh in (0, 1):
@@ -418,27 +422,32 @@
     copy.start()
     plane_faces(params, pf_ref, BLK, 0)
 
-    def collect(i, n):
-        todo_ref[n] = meta_ref[PARTS * SLOTS + i]
-        return n + meta_ref[i]
-
-    count = lax.fori_loop(0, PARTS * SLOTS, collect, 0, unroll=8)
-    for extra in range(4):
-        todo_ref[count + extra] = 0
-    todo_ref[TODO - 1] = count
+    for todo_ref, first, parts in ((early_ref, 0, EARLY), (late_ref, EARLY, PARTS - EARLY)):
+
+        def collect(i, n, todo_ref=todo_ref):
+            todo_ref[n] = meta_ref[PARTS * SLOTS + i]
+            return n + meta_ref[i]
+
+        begin = first * SLOTS
+        count = lax.fori_loop(begin, begin + parts * SLOTS, collect, 0, unroll=8)
+        for extra in range(4):
+            todo_ref[count + extra] = begin
+        todo_ref[TODO - 1] = count
     copy.wait()
 
 
-def moment_kernel(
-    todo, pf_ref, speed_ref, s0_ref, s1_ref, s2_ref, s3_ref, s4_ref, s5_ref, out_ref, slots
-):
+def moment_kernel(first, todo, pf_ref, speed_ref, *rest):
+    *parts, out_ref, slots = rest
     lane = lane_ids()
     row = row_ids()
-    out_ref[...] = jnp.zeros_like(out_ref)
-    for at, ref in enumerate((s0_ref, s1_ref, s2_ref, s3_ref, s4_ref, s5_ref)):
+    if first == 0:
+        out_ref[...] = jnp.zeros_like(out_ref)
+    else:
+        *parts, before_ref = parts
+        out_ref[...] = before_ref[...]
+    for at, ref in enumerate(parts):
         for u in range(12):
             slots[at * 12 + u] = ref[u]
-
     count = todo[TODO - 1]
     quarter = lane // 32
     first_off = (((lane // 16) % 2).astype(jnp.float32) - 0.5) * 0.5
@@ -464,7 +473,8 @@
             axis = lax.shift_right_logical(k, 1)
             qa = lax.shift_right_logical(quad, 1)
             qb = quad & 1
-            held = lax.shift_right_logical(i, 4) * 12 + (lax.shift_right_logical(i, 2) & 3)
+            part = lax.shift_right_logical(i, 4) - first
+            held = part * 12 + (lax.shift_right_logical(i, 2) & 3)
             turn = (i & 3) * 32 + lane % 32
             for comp in range(3):
                 fine[comp] = merge(fine[comp], pick(slots[held + 4 * comp], turn), q)
@@ -598,17 +608,19 @@
     points, speed = pl.pallas_call(
         prepare_kernel,
         out_shape=(pltpu.HBM((7, 4, 256, LANES), f32), out((BLK, 16, LANES))),
-        in_specs=[VMEM_SPEC] * 2,
+        in_specs=[VMEM_SPEC, hbm],
         out_specs=(hbm, VMEM_SPEC),
         scratch_shapes=[
             pltpu.VMEM((4, 2, 32, LANES), f32),
             pltpu.VMEM((7, 4, 256, LANES), f32),
+            pltpu.VMEM((3, 256, LANES), f32),
+            pltpu.SemaphoreType.DMA,
             pltpu.SemaphoreType.DMA,
         ],
         compiler_params=limit,
         cost_estimate=lasting(4),
         name="prepare",
-    )(field, velo)
+    )(field, pltpu.with_memory_space_constraint(velo, pltpu.HBM))
     points = pltpu.with_memory_space_constraint(points, pltpu.HBM)
     params, slots = pl.pallas_call(
         fit_kernel,
@@ -644,32 +656,34 @@
     )
     meta = jnp.stack([mine.astype(i32), entry]).reshape(2 * PARTS * SLOTS)
 
-    planes, plane_face, todo = pl.pallas_call(
+    todo = jax.ShapeDtypeStruct((TODO,), i32)
+    planes, plane_face, early, late = pl.pallas_call(
         emit_kernel,
-        out_shape=(
-            out((1024, LANES)),
-            out((BLK * 4, 16, LANES)),
-            jax.ShapeDtypeStruct((TODO,), i32),
-        ),
+        out_shape=(out((1024, LANES)), out((BLK * 4, 16, LANES)), todo, todo),
         in_specs=[SMEM_SPEC, VMEM_SPEC],
-        out_specs=(hbm, VMEM_SPEC, SMEM_SPEC),
+        out_specs=(hbm, VMEM_SPEC, SMEM_SPEC, SMEM_SPEC),
         scratch_shapes=[pltpu.VMEM((1024, LANES), f32), pltpu.SemaphoreType.DMA],
         compiler_params=limit,
         cost_estimate=lasting(2),
         name="emit",
     )(meta, params)
     plane_face, near, far = lax.optimization_barrier((plane_face, *got_slots[1:]))
-    got_slots = [got_slots[0], near, far] + relay([near, far])
-
-    reflux = pl.pallas_call(
-        moment_kernel,
-        out_shape=out((BLK * 6 * 4, LANES)),
-        in_specs=[SMEM_SPEC] + [VMEM_SPEC] * 8,
-        out_specs=VMEM_SPEC,
-        scratch_shapes=[pltpu.VMEM((PARTS * 12, 8, LANES), f32)],
-        compiler_params=limit,
-        name="moments",
-    )(todo, plane_face, speed, slots, *got_slots)
+    others = relay([near, far])
+
+    def moments(first, todo, *operands):
+        return pl.pallas_call(
+            functools.partial(moment_kernel, first),
+            out_shape=out((BLK * 6 * 4, LANES)),
+            in_specs=[SMEM_SPEC] + [VMEM_SPEC] * (2 + len(operands)),
+            out_specs=VMEM_SPEC,
+            scratch_shapes=[pltpu.VMEM((EARLY * 12, 8, LANES), f32)],
+            compiler_params=limit,
+            cost_estimate=lasting(2),
+            name="moments",
+        )(todo, plane_face, speed, *operands)
+
+    reflux = moments(0, early, slots, got_slots[0], near, far)
+    reflux = moments(EARLY, late, *others, reflux)
 
     planes = planes.reshape(BLK, 32, 4, LANES).transpose(0, 2, 1, 3).reshape(BLK, 4, 4096)
     reflux = reflux.reshape(BLK, 6, 2, 2, LANES).transpose(0, 1, 3, 2, 4).reshape(BLK, 6, 2, 256)

time: 44.8 us -> 44.3 us (0.989); the launches traced: 44.3 us -> 44.3 us
  Pallas kernels: 21.7 us -> 22.7 us
  local copies, waits for them, and re-layouts: 1.33 us -> 0.34 us
  starting transfers between devices: 17.3 us -> 18 us
  waiting for transfers between devices: 2.97 us -> 2.29 us
    unnamed x3 -> x1, local copies, waits for them, and re-layouts: 1 us -> 0.01 us
    ppermute x4, waiting for transfers between devices: 2.26 us -> 1.27 us  [relay(): return [lax.ppermute(value, 'sfc', inside) for value in values]]
    pallas_call x1 -> x2, Pallas kernels: 2.05 us -> 3.02 us  [moments(): pl.pallas_call(functools.partial(moment_kernel, first), out_shape=out((BL...]
    ppermute x4, starting transfers between devices: 3.38 us -> 4.05 us  [relay(): return [lax.ppermute(value, 'sfc', inside) for value in values]]
  transfers between devices with their start and end apart: 10 -> 10, of which waited for: 5 -> 5; matrix products, arithmetic and copies ran while one was open for 1% -> 1% of each run, Pallas kernels for 12% -> 14%
where the time goes in v4:
time: 44.3 us
  Pallas kernels  22.7 us (51%)
  starting transfers between devices  18 us (41%)
  waiting for transfers between devices  2.29 us (5%)
  between operations  0.73 us (2%)
    pallas_call x1, Pallas kernels, per_device(): pl.pallas_call(fit_kernel, out_shape=(out((4, 256, LANES)), out((12, 8, L...  12.8 us
    ppermute x2, starting transfers between devices, trade(): far = lax.ppermute(value, 'sfc', partners(n, 2, 2))  12.5 us
    ppermute x4, starting transfers between devices, relay(): return [lax.ppermute(value, 'sfc', inside) for value in values]  4.05 us
    pallas_call x1, Pallas kernels, per_device(): pl.pallas_call(prepare_kernel, out_shape=(pltpu.HBM((7, 4, 256, LANES), f...  3.03 us
    pallas_call x2, Pallas kernels, moments(): pl.pallas_call(functools.partial(moment_kernel, first), out_shape=out((BL...  3.02 us
    pallas_call x1, Pallas kernels, per_device(): pl.pallas_call(emit_kernel, out_shape=(out((1024, LANES)), out((BLK * 4,...  2.29 us
    pallas_call x1, Pallas kernels, per_device(): pl.pallas_call(pack_kernel, out_shape=(out((49, 8, LANES)), out((4, 256,...  1.48 us
    ppermute x2, starting transfers between devices, trade(): return [lax.ppermute(value, 'sfc', partners(n, 1, 0)), near, far]  1.42 us
  transfers between devices with their start and end apart: 10, of which 5 were waited for; matrix products, arithmetic and copies ran while one was open for 1% of the time, Pallas kernels for 14%

profile of v4, /device:TPU:25, one launch (start us, length us, event | category | flops | bytes accessed | tf_op | source)
XLA Modules:
  0.0 44.3 jit_solution(8939027053255688347)
XLA Ops:
  0.6 1.5 %pack.1 = (f32[49,8,128]{2,1,0:T(8,128)S(1)}, f32[4,256,128]{2,1,0:T(8,128)S(1)}, s32[4,16]{1,0:T(4,128)S(1)}, s32[8,6]{1,0:T(8,128)S(1)}) custom-call(f32[256,128]{1,0:T(8,128)} %bitcast.54, f32[3,256,128]{2,1,0:T(8,128)} %bitcast.53, s32[4,16]{1,0:T(4,128)} %bitcast.56, s32[8,6]{1,0:T(8,128)} %near_hbm.1), custom_call_target="tpu_custom_call" | custom-call | tf_op jit(solution)/shard_map/pack/pallas_call | solution.py:571
  2.1 8.0 %collective-permute-start.2 = (f32[49,8,128]{2,1,0:T(8,128)S(1)}, f32[49,8,128]{2,1,0:T(8,128)S(1)}, u32[]{:S(2)}, u32[]{:S(2)}) collective-permute-start(f32[49,8,128]{2,1,0:T(8,128)S(1)} %get-tuple-element.18.own_ref), channel_id=1, source_target_pairs={{0,1},{1,0},{2,4},{3,5},{4,2},{5,3},{6,8},{7,9},{8,6},{9,7},{10,12... | collective-permute-start | bytes 602120 | tf_op jit(solution)/shard_map/ppermute | solution.py:540
  10.2 0.0 collective-permute-start.1
  10.2 1.0 %collective-permute-start = (f32[49,8,128]{2,1,0:T(8,128)S(1)}, f32[49,8,128]{2,1,0:T(8,128)S(1)}, u32[]{:S(2)}, u32[]{:S(2)}) collective-permute-start(f32[49,8,128]{2,1,0:T(8,128)S(1)} %get-tuple-element.18.own_ref), channel_id=1, source_target_pairs={{0,1},{1,0},{2,3},{3,2},{4,5},{5,4},{6,7},{7,6},{8,9},{9,8},{10,11... | collective-permute-start | bytes 602120 | tf_op jit(solution)/shard_map/ppermute | solution.py:542
  11.1 0.1 select_clamp_fusion
  11.2 0.1 reshape.195.tbl_ref
  11.3 0.1 copy.11
  11.4 0.1 reshape.196.refine_ref
  11.5 3.0 %prepare.1 = (f32[7,4,256,128]{3,2,1,0:T(8,128)}, f32[8,16,128]{2,1,0:T(8,128)S(1)}) custom-call(f32[4,256,128]{2,1,0:T(8,128)S(1)} %get-tuple-element.20.field, f32[3,256,128]{2,1,0:T(8,128)} %bitcast.52), custom_call_target="tpu_custom_call" | custom-call | bytes 14000000 | tf_op jit(solution)/shard_map/prepare/pallas_call | solution.py:608
  14.6 0.3 collective-permute-done.2.r3_ref
  14.9 1.2 %collective-permute-start.4 = (f32[49,8,128]{2,1,0:T(8,128)S(1)}, f32[49,8,128]{2,1,0:T(8,128)S(1)}, u32[]{:S(2)}, u32[]{:S(2)}) collective-permute-start(f32[49,8,128]{2,1,0:T(8,128)S(1)} %collective-permute-done.2.r3_ref), channel_id=1, source_target_pairs={{0,1},{1,0},{2,3},{3,2},{4,5},{5,4},{6,7},{7,6},{8,9},{9,8},{10,11... | collective-permute-start | bytes 602120 | tf_op jit(solution)/shard_map/ppermute | solution.py:547
  16.1 0.0 collective-permute-done.1.r2_ref
  16.1 1.5 %collective-permute-start.3 = (f32[49,8,128]{2,1,0:T(8,128)S(1)}, f32[49,8,128]{2,1,0:T(8,128)S(1)}, u32[]{:S(2)}, u32[]{:S(2)}) collective-permute-start(f32[49,8,128]{2,1,0:T(8,128)S(1)} %collective-permute-done.1.r2_ref), channel_id=1, source_target_pairs={{0,1},{1,0},{2,3},{3,2},{4,5},{5,4},{6,7},{7,6},{8,9},{9,8},{10,11... | collective-permute-start | bytes 602120 | tf_op jit(solution)/shard_map/ppermute | solution.py:547
  17.6 0.0 collective-permute-done.r1_ref
  17.6 0.0 collective-permute-done.4.r5_ref
  17.6 1.0 %collective-permute-done.3.r4_ref = f32[49,8,128]{2,1,0:T(8,128)S(1)} collective-permute-done((f32[49,8,128]{2,1,0:T(8,128)S(1)}, f32[49,8,128]{2,1,0:T(8,128)S(1)}, u32[]{:S(2)}, u32[]{:S(2)}) %collective-permute-start.3) | collective-permute-done | bytes 200736 | tf_op jit(solution)/shard_map/ppermute | solution.py:547
  18.6 12.8 %fit.1 = (f32[4,256,128]{2,1,0:T(8,128)S(1)}, f32[12,8,128]{2,1,0:T(8,128)S(1)}) custom-call(s32[48]{0:T(128)S(1)} %reshape.195.tbl_ref, s32[32]{0:T(128)S(1)} %reshape.196.refine_ref, f32[49,8,128]{2,1,0:T(8,128)S(1)} %get-tuple-element.18.own_ref, f32[49,8,128]{2,1,0:T(8,128)S(1)} %collective-permute-done.r1_ref, ...), custom_call_target="tpu_custom_call" | custom-call | bytes 42000000 | tf_op jit(solution)/shard_map/fit/pallas_call | solution.py:625
  31.5 0.5 %collective-permute-start.9 = (f32[12,8,128]{2,1,0:T(8,128)S(1)}, f32[12,8,128]{2,1,0:T(8,128)S(1)}, u32[]{:S(2)}, u32[]{:S(2)}) collective-permute-start(f32[12,8,128]{2,1,0:T(8,128)S(1)} %get-tuple-element.27.rest_0_), channel_id=1, source_target_pairs={{0,1},{1,0},{2,3},{3,2},{4,5},{5,4},{6,7},{7,6},{8,9},{9,8},{10,11... | collective-permute-start | bytes 147464 | tf_op jit(solution)/shard_map/ppermute | solution.py:542
  31.9 4.5 %collective-permute-start.6 = (f32[12,8,128]{2,1,0:T(8,128)S(1)}, f32[12,8,128]{2,1,0:T(8,128)S(1)}, u32[]{:S(2)}, u32[]{:S(2)}) collective-permute-start(f32[12,8,128]{2,1,0:T(8,128)S(1)} %get-tuple-element.27.rest_0_), channel_id=1, source_target_pairs={{0,1},{1,0},{2,4},{3,5},{4,2},{5,3},{6,8},{7,9},{8,6},{9,7},{10,12... | collective-permute-start | bytes 147464 | tf_op jit(solution)/shard_map/ppermute | solution.py:540
  36.5 0.0 collective-permute-start.5
  36.5 0.1 and_convert_fusion
  36.6 0.1 reshape.194.meta_ref
  36.7 2.3 %emit.1 = (f32[1024,128]{1,0:T(8,128)}, f32[32,16,128]{2,1,0:T(8,128)S(1)}, s32[112]{0:T(128)S(1)}, s32[112]{0:T(128)S(1)}) custom-call(s32[192]{0:T(256)S(1)} %reshape.194.meta_ref, f32[4,256,128]{2,1,0:T(8,128)S(1)} %get-tuple-element.23.params), custom_call_target="tpu_custom_call" | custom-call | bytes 7000000 | tf_op jit(solution)/shard_map/emit/pallas_call | solution.py:660
  39.0 0.1 collective-permute-done.6.rest_3_
  39.1 0.6 %collective-permute-done.5.rest_2_ = f32[12,8,128]{2,1,0:T(8,128)S(1)} collective-permute-done((f32[12,8,128]{2,1,0:T(8,128)S(1)}, f32[12,8,128]{2,1,0:T(8,128)S(1)}, u32[]{:S(2)}, u32[]{:S(2)}) %collective-permute-start.5) | collective-permute-done | bytes 49184 | tf_op jit(solution)/shard_map/ppermute | solution.py:541
  39.7 1.4 %collective-permute-start.7 = (f32[12,8,128]{2,1,0:T(8,128)S(1)}, f32[12,8,128]{2,1,0:T(8,128)S(1)}, u32[]{:S(2)}, u32[]{:S(2)}) collective-permute-start(f32[12,8,128]{2,1,0:T(8,128)S(1)} %collective-permute-done.5.rest_2_), channel_id=1, source_target_pairs={{0,1},{1,0},{2,3},{3,2},{4,5},{5,4},{6,7},{7,6},{8,9},{9,8},{10,11... | collective-permute-start | bytes 147464 | tf_op jit(solution)/shard_map/ppermute | solution.py:547
  41.0 0.0 collective-permute-start.8
  41.1 0.0 collective-permute-done.9.rest_1_
  41.1 1.0 %moments.2.rest_2_ = f32[192,128]{1,0:T(8,128)S(1)} custom-call(s32[112]{0:T(128)S(1)} %get-tuple-element.31.todo, f32[32,16,128]{2,1,0:T(8,128)S(1)} %get-tuple-element.28.pf_ref, f32[8,16,128]{2,1,0:T(8,128)S(1)} %get-tuple-element.22.speed_ref, f32[12,8,128]{2,1,0:T(8,128)S(1)} %get-tuple-element.27.rest_0_, ...), custom_call_target="tpu_custom_call" | custom-call | bytes 7000000 | tf_op jit(solution)/shard_map/moments/pallas_call | solution.py:674
  42.0 0.0 collective-permute-done.7.rest_0_
  42.1 0.2 collective-permute-done.8.rest_1_
  42.3 2.0 %moments.3 = f32[192,128]{1,0:T(8,128)} custom-call(s32[112]{0:T(128)S(1)} %get-tuple-element.25.todo, f32[32,16,128]{2,1,0:T(8,128)S(1)} %get-tuple-element.28.pf_ref, f32[8,16,128]{2,1,0:T(8,128)S(1)} %get-tuple-element.22.speed_ref, f32[12,8,128]{2,1,0:T(8,128)S(1)} %collective-permute-done.7.rest_0_, f32[12,8,128]{2,1,0:T(8,128)S(1)} %collective-permute-done.8.rest_1_, ...), custom_call_target="tpu_custom_call" | custom-call | bytes 7000000 | tf_op jit(solution)/shard_map/moments/pallas_call | solution.py:674
  (14 shorter events, 0.1 us)
Async XLA Ops:
  2.1 12.8 %collective-permute-start.2 = (f32[49,8,128]{2,1,0:T(8,128)S(1)}, f32[49,8,128]{2,1,0:T(8,128)S(1)}, u32[]{:S(2)}, u32[]{:S(2)}) collective-permute-start(f32[49,8,128]{2,1,0:T(8,128)S(1)} %get-tuple-element.18.own_ref), channel_id=1, source_target_pairs={{0,1},{1,0},{2,4},{3,5},{4,2},{5,3},{6,8},{7,9},{8,6},{9,7},{10,12... | collective-permute-start | bytes 602120 | tf_op jit(solution)/shard_map/ppermute | solution.py:540
  10.2 5.9 %collective-permute-start.1 = (f32[49,8,128]{2,1,0:T(8,128)S(1)}, f32[49,8,128]{2,1,0:T(8,128)S(1)}, u32[]{:S(2)}, u32[]{:S(2)}) collective-permute-start(f32[49,8,128]{2,1,0:T(8,128)S(1)} %get-tuple-element.18.own_ref), channel_id=1, source_target_pairs={{0,2},{1,3},{2,0},{3,1},{4,6},{5,7},{6,4},{7,5},{8,10},{9,11},{10,... | collective-permute-start | bytes 602120 | tf_op jit(solution)/shard_map/ppermute | solution.py:541
  10.2 7.4 %collective-permute-start = (f32[49,8,128]{2,1,0:T(8,128)S(1)}, f32[49,8,128]{2,1,0:T(8,128)S(1)}, u32[]{:S(2)}, u32[]{:S(2)}) collective-permute-start(f32[49,8,128]{2,1,0:T(8,128)S(1)} %get-tuple-element.18.own_ref), channel_id=1, source_target_pairs={{0,1},{1,0},{2,3},{3,2},{4,5},{5,4},{6,7},{7,6},{8,9},{9,8},{10,11... | collective-permute-start | bytes 602120 | tf_op jit(solution)/shard_map/ppermute | solution.py:542
  14.9 2.7 %collective-permute-start.4 = (f32[49,8,128]{2,1,0:T(8,128)S(1)}, f32[49,8,128]{2,1,0:T(8,128)S(1)}, u32[]{:S(2)}, u32[]{:S(2)}) collective-permute-start(f32[49,8,128]{2,1,0:T(8,128)S(1)} %collective-permute-done.2.r3_ref), channel_id=1, source_target_pairs={{0,1},{1,0},{2,3},{3,2},{4,5},{5,4},{6,7},{7,6},{8,9},{9,8},{10,11... | collective-permute-start | bytes 602120 | tf_op jit(solution)/shard_map/ppermute | solution.py:547
  16.1 2.5 %collective-permute-start.3 = (f32[49,8,128]{2,1,0:T(8,128)S(1)}, f32[49,8,128]{2,1,0:T(8,128)S(1)}, u32[]{:S(2)}, u32[]{:S(2)}) collective-permute-start(f32[49,8,128]{2,1,0:T(8,128)S(1)} %collective-permute-done.1.r2_ref), channel_id=1, source_target_pairs={{0,1},{1,0},{2,3},{3,2},{4,5},{5,4},{6,7},{7,6},{8,9},{9,8},{10,11... | collective-permute-start | bytes 602120 | tf_op jit(solution)/shard_map/ppermute | solution.py:547
  31.5 9.6 %collective-permute-start.9 = (f32[12,8,128]{2,1,0:T(8,128)S(1)}, f32[12,8,128]{2,1,0:T(8,128)S(1)}, u32[]{:S(2)}, u32[]{:S(2)}) collective-permute-start(f32[12,8,128]{2,1,0:T(8,128)S(1)} %get-tuple-element.27.rest_0_), channel_id=1, source_target_pairs={{0,1},{1,0},{2,3},{3,2},{4,5},{5,4},{6,7},{7,6},{8,9},{9,8},{10,11... | collective-permute-start | bytes 147464 | tf_op jit(solution)/shard_map/ppermute | solution.py:542
  31.9 7.2 %collective-permute-start.6 = (f32[12,8,128]{2,1,0:T(8,128)S(1)}, f32[12,8,128]{2,1,0:T(8,128)S(1)}, u32[]{:S(2)}, u32[]{:S(2)}) collective-permute-start(f32[12,8,128]{2,1,0:T(8,128)S(1)} %get-tuple-element.27.rest_0_), channel_id=1, source_target_pairs={{0,1},{1,0},{2,4},{3,5},{4,2},{5,3},{6,8},{7,9},{8,6},{9,7},{10,12... | collective-permute-start | bytes 147464 | tf_op jit(solution)/shard_map/ppermute | solution.py:540
  36.5 3.2 %collective-permute-start.5 = (f32[12,8,128]{2,1,0:T(8,128)S(1)}, f32[12,8,128]{2,1,0:T(8,128)S(1)}, u32[]{:S(2)}, u32[]{:S(2)}) collective-permute-start(f32[12,8,128]{2,1,0:T(8,128)S(1)} %get-tuple-element.27.rest_0_), channel_id=1, source_target_pairs={{0,2},{1,3},{2,0},{3,1},{4,6},{5,7},{6,4},{7,5},{8,10},{9,11},{10,... | collective-permute-start | bytes 147464 | tf_op jit(solution)/shard_map/ppermute | solution.py:541
  39.7 2.4 %collective-permute-start.7 = (f32[12,8,128]{2,1,0:T(8,128)S(1)}, f32[12,8,128]{2,1,0:T(8,128)S(1)}, u32[]{:S(2)}, u32[]{:S(2)}) collective-permute-start(f32[12,8,128]{2,1,0:T(8,128)S(1)} %collective-permute-done.5.rest_2_), channel_id=1, source_target_pairs={{0,1},{1,0},{2,3},{3,2},{4,5},{5,4},{6,7},{7,6},{8,9},{9,8},{10,11... | collective-permute-start | bytes 147464 | tf_op jit(solution)/shard_map/ppermute | solution.py:547
  41.0 1.2 %collective-permute-start.8 = (f32[12,8,128]{2,1,0:T(8,128)S(1)}, f32[12,8,128]{2,1,0:T(8,128)S(1)}, u32[]{:S(2)}, u32[]{:S(2)}) collective-permute-start(f32[12,8,128]{2,1,0:T(8,128)S(1)} %collective-permute-done.6.rest_3_), channel_id=1, source_target_pairs={{0,1},{1,0},{2,3},{3,2},{4,5},{5,4},{6,7},{7,6},{8,9},{9,8},{10,11... | collective-permute-start | bytes 147464 | tf_op jit(solution)/shard_map/ppermute | solution.py:547

commit v5 on v4

--- a/solution.py
+++ b/solution.py
@@ -356,7 +356,7 @@
             slots_ref[4 * comp + g] = total[comp]
         return carry
 
-    lax.fori_loop(0, SLOTS // 4, tile, 0, unroll=2)
+    lax.fori_loop(0, SLOTS // 4, tile, 0, unroll=True)
 
 
 def fit_kernel(
@@ -379,7 +379,7 @@
                 table[at * 48 + i * 12 + u] = ref[i * 12 + u]
             return carry
 
-        lax.fori_loop(0, 4, copy, 0)
+        lax.fori_loop(0, 4, copy, 0, unroll=True)
 
     def swap(i, carry):
         for u in range(2, 6):
@@ -390,7 +390,7 @@
             )
         return carry
 
-    lax.fori_loop(0, BLK, swap, 0, unroll=2)
+    lax.fori_loop(0, BLK, swap, 0, unroll=True)
     for b in range(BLK):
         fetches[b].wait()
         if b + 2 < BLK:

time: 44.3 us -> 44 us (level); the launches traced: 44.3 us -> 43.4 us
  Pallas kernels: 22.7 us -> 21.6 us
    pallas_call x2, Pallas kernels: 3.02 us -> 2.18 us  [moments(): pl.pallas_call(functools.partial(moment_kernel, first), out_shape=out((BL...]
  transfers between devices with their start and end apart: 10 -> 10, of which waited for: 5 -> 5; matrix products, arithmetic and copies ran while one was open for 1% -> 1% of each run, Pallas kernels for 14% -> 15%
where the time goes in v5:
time: 44 us; the launch traced here: 43.4 us
  Pallas kernels  21.6 us (49%)
  starting transfers between devices  18.1 us (41%)
  waiting for transfers between devices  2.29 us (5%)
  between operations  0.73 us (2%)
    pallas_call x1, Pallas kernels, per_device(): pl.pallas_call(fit_kernel, out_shape=(out((4, 256, LANES)), out((12, 8, L...  12.6 us
    ppermute x2, starting transfers between devices, trade(): far = lax.ppermute(value, 'sfc', partners(n, 2, 2))  12.6 us
    ppermute x4, starting transfers between devices, relay(): return [lax.ppermute(value, 'sfc', inside) for value in values]  4.1 us
    pallas_call x1, Pallas kernels, per_device(): pl.pallas_call(prepare_kernel, out_shape=(pltpu.HBM((7, 4, 256, LANES), f...  3.03 us
    pallas_call x1, Pallas kernels, per_device(): pl.pallas_call(emit_kernel, out_shape=(out((1024, LANES)), out((BLK * 4,...  2.29 us
    pallas_call x2, Pallas kernels, moments(): pl.pallas_call(functools.partial(moment_kernel, first), out_shape=out((BL...  2.18 us
    pallas_call x1, Pallas kernels, per_device(): pl.pallas_call(pack_kernel, out_shape=(out((49, 8, LANES)), out((4, 256,...  1.48 us
    ppermute x2, starting transfers between devices, trade(): return [lax.ppermute(value, 'sfc', partners(n, 1, 0)), near, far]  1.41 us
  transfers between devices with their start and end apart: 10, of which 5 were waited for; matrix products, arithmetic and copies ran while one was open for 1% of the time, Pallas kernels for 15%

profile of v5, /device:TPU:25, one launch (start us, length us, event | category | flops | bytes accessed | tf_op | source)
XLA Modules:
  0.0 43.4 jit_solution(17377843315656569719)
XLA Ops:
  0.6 1.5 %pack.1 = (f32[49,8,128]{2,1,0:T(8,128)S(1)}, f32[4,256,128]{2,1,0:T(8,128)S(1)}, s32[4,16]{1,0:T(4,128)S(1)}, s32[8,6]{1,0:T(8,128)S(1)}) custom-call(f32[256,128]{1,0:T(8,128)} %bitcast.54, f32[3,256,128]{2,1,0:T(8,128)} %bitcast.53, s32[4,16]{1,0:T(4,128)} %bitcast.56, s32[8,6]{1,0:T(8,128)} %near_hbm.1), custom_call_target="tpu_custom_call" | custom-call | tf_op jit(solution)/shard_map/pack/pallas_call | solution.py:571
  2.1 8.0 %collective-permute-start.2 = (f32[49,8,128]{2,1,0:T(8,128)S(1)}, f32[49,8,128]{2,1,0:T(8,128)S(1)}, u32[]{:S(2)}, u32[]{:S(2)}) collective-permute-start(f32[49,8,128]{2,1,0:T(8,128)S(1)} %get-tuple-element.18.own_ref), channel_id=1, source_target_pairs={{0,1},{1,0},{2,4},{3,5},{4,2},{5,3},{6,8},{7,9},{8,6},{9,7},{10,12... | collective-permute-start | bytes 602120 | tf_op jit(solution)/shard_map/ppermute | solution.py:540
  10.2 0.0 collective-permute-start.1
  10.2 1.0 %collective-permute-start = (f32[49,8,128]{2,1,0:T(8,128)S(1)}, f32[49,8,128]{2,1,0:T(8,128)S(1)}, u32[]{:S(2)}, u32[]{:S(2)}) collective-permute-start(f32[49,8,128]{2,1,0:T(8,128)S(1)} %get-tuple-element.18.own_ref), channel_id=1, source_target_pairs={{0,1},{1,0},{2,3},{3,2},{4,5},{5,4},{6,7},{7,6},{8,9},{9,8},{10,11... | collective-permute-start | bytes 602120 | tf_op jit(solution)/shard_map/ppermute | solution.py:542
  11.1 0.1 select_clamp_fusion
  11.2 0.1 reshape.195.tbl_ref
  11.3 0.1 copy.11
  11.4 0.1 reshape.196.refine_ref
  11.5 3.0 %prepare.1 = (f32[7,4,256,128]{3,2,1,0:T(8,128)}, f32[8,16,128]{2,1,0:T(8,128)S(1)}) custom-call(f32[4,256,128]{2,1,0:T(8,128)S(1)} %get-tuple-element.20.field, f32[3,256,128]{2,1,0:T(8,128)} %bitcast.52), custom_call_target="tpu_custom_call" | custom-call | bytes 14000000 | tf_op jit(solution)/shard_map/prepare/pallas_call | solution.py:608
  14.6 0.3 collective-permute-done.2.r3_ref
  14.9 1.2 %collective-permute-start.4 = (f32[49,8,128]{2,1,0:T(8,128)S(1)}, f32[49,8,128]{2,1,0:T(8,128)S(1)}, u32[]{:S(2)}, u32[]{:S(2)}) collective-permute-start(f32[49,8,128]{2,1,0:T(8,128)S(1)} %collective-permute-done.2.r3_ref), channel_id=1, source_target_pairs={{0,1},{1,0},{2,3},{3,2},{4,5},{5,4},{6,7},{7,6},{8,9},{9,8},{10,11... | collective-permute-start | bytes 602120 | tf_op jit(solution)/shard_map/ppermute | solution.py:547
  16.1 0.0 collective-permute-done.1.r2_ref
  16.1 1.5 %collective-permute-start.3 = (f32[49,8,128]{2,1,0:T(8,128)S(1)}, f32[49,8,128]{2,1,0:T(8,128)S(1)}, u32[]{:S(2)}, u32[]{:S(2)}) collective-permute-start(f32[49,8,128]{2,1,0:T(8,128)S(1)} %collective-permute-done.1.r2_ref), channel_id=1, source_target_pairs={{0,1},{1,0},{2,3},{3,2},{4,5},{5,4},{6,7},{7,6},{8,9},{9,8},{10,11... | collective-permute-start | bytes 602120 | tf_op jit(solution)/shard_map/ppermute | solution.py:547
  17.6 0.0 collective-permute-done.r1_ref
  17.6 0.0 collective-permute-done.4.r5_ref
  17.6 1.0 %collective-permute-done.3.r4_ref = f32[49,8,128]{2,1,0:T(8,128)S(1)} collective-permute-done((f32[49,8,128]{2,1,0:T(8,128)S(1)}, f32[49,8,128]{2,1,0:T(8,128)S(1)}, u32[]{:S(2)}, u32[]{:S(2)}) %collective-permute-start.3) | collective-permute-done | bytes 200736 | tf_op jit(solution)/shard_map/ppermute | solution.py:547
  18.6 12.6 %fit.1 = (f32[4,256,128]{2,1,0:T(8,128)S(1)}, f32[12,8,128]{2,1,0:T(8,128)S(1)}) custom-call(s32[48]{0:T(128)S(1)} %reshape.195.tbl_ref, s32[32]{0:T(128)S(1)} %reshape.196.refine_ref, f32[49,8,128]{2,1,0:T(8,128)S(1)} %get-tuple-element.18.own_ref, f32[49,8,128]{2,1,0:T(8,128)S(1)} %collective-permute-done.r1_ref, ...), custom_call_target="tpu_custom_call" | custom-call | bytes 42000000 | tf_op jit(solution)/shard_map/fit/pallas_call | solution.py:625
  31.3 0.5 %collective-permute-start.9 = (f32[12,8,128]{2,1,0:T(8,128)S(1)}, f32[12,8,128]{2,1,0:T(8,128)S(1)}, u32[]{:S(2)}, u32[]{:S(2)}) collective-permute-start(f32[12,8,128]{2,1,0:T(8,128)S(1)} %get-tuple-element.27.rest_0_), channel_id=1, source_target_pairs={{0,1},{1,0},{2,3},{3,2},{4,5},{5,4},{6,7},{7,6},{8,9},{9,8},{10,11... | collective-permute-start | bytes 147464 | tf_op jit(solution)/shard_map/ppermute | solution.py:542
  31.7 4.5 %collective-permute-start.6 = (f32[12,8,128]{2,1,0:T(8,128)S(1)}, f32[12,8,128]{2,1,0:T(8,128)S(1)}, u32[]{:S(2)}, u32[]{:S(2)}) collective-permute-start(f32[12,8,128]{2,1,0:T(8,128)S(1)} %get-tuple-element.27.rest_0_), channel_id=1, source_target_pairs={{0,1},{1,0},{2,4},{3,5},{4,2},{5,3},{6,8},{7,9},{8,6},{9,7},{10,12... | collective-permute-start | bytes 147464 | tf_op jit(solution)/shard_map/ppermute | solution.py:540
  36.3 0.0 collective-permute-start.5
  36.3 0.1 and_convert_fusion
  36.4 0.1 reshape.194.meta_ref
  36.5 2.3 %emit.1 = (f32[1024,128]{1,0:T(8,128)}, f32[32,16,128]{2,1,0:T(8,128)S(1)}, s32[112]{0:T(128)S(1)}, s32[112]{0:T(128)S(1)}) custom-call(s32[192]{0:T(256)S(1)} %reshape.194.meta_ref, f32[4,256,128]{2,1,0:T(8,128)S(1)} %get-tuple-element.23.params), custom_call_target="tpu_custom_call" | custom-call | bytes 7000000 | tf_op jit(solution)/shard_map/emit/pallas_call | solution.py:660
  38.8 0.1 collective-permute-done.6.rest_3_
  38.9 0.6 %collective-permute-done.5.rest_2_ = f32[12,8,128]{2,1,0:T(8,128)S(1)} collective-permute-done((f32[12,8,128]{2,1,0:T(8,128)S(1)}, f32[12,8,128]{2,1,0:T(8,128)S(1)}, u32[]{:S(2)}, u32[]{:S(2)}) %collective-permute-start.5) | collective-permute-done | bytes 49184 | tf_op jit(solution)/shard_map/ppermute | solution.py:541
  39.5 1.4 %collective-permute-start.7 = (f32[12,8,128]{2,1,0:T(8,128)S(1)}, f32[12,8,128]{2,1,0:T(8,128)S(1)}, u32[]{:S(2)}, u32[]{:S(2)}) collective-permute-start(f32[12,8,128]{2,1,0:T(8,128)S(1)} %collective-permute-done.5.rest_2_), channel_id=1, source_target_pairs={{0,1},{1,0},{2,3},{3,2},{4,5},{5,4},{6,7},{7,6},{8,9},{9,8},{10,11... | collective-permute-start | bytes 147464 | tf_op jit(solution)/shard_map/ppermute | solution.py:547
  40.9 0.0 collective-permute-start.8
  40.9 0.0 collective-permute-done.9.rest_1_
  40.9 1.0 %moments.2.rest_2_ = f32[192,128]{1,0:T(8,128)S(1)} custom-call(s32[112]{0:T(128)S(1)} %get-tuple-element.31.todo, f32[32,16,128]{2,1,0:T(8,128)S(1)} %get-tuple-element.28.pf_ref, f32[8,16,128]{2,1,0:T(8,128)S(1)} %get-tuple-element.22.speed_ref, f32[12,8,128]{2,1,0:T(8,128)S(1)} %get-tuple-element.27.rest_0_, ...), custom_call_target="tpu_custom_call" | custom-call | bytes 7000000 | tf_op jit(solution)/shard_map/moments/pallas_call | solution.py:674
  41.9 0.0 collective-permute-done.7.rest_0_
  41.9 0.2 collective-permute-done.8.rest_1_
  42.2 1.2 %moments.3 = f32[192,128]{1,0:T(8,128)} custom-call(s32[112]{0:T(128)S(1)} %get-tuple-element.25.todo, f32[32,16,128]{2,1,0:T(8,128)S(1)} %get-tuple-element.28.pf_ref, f32[8,16,128]{2,1,0:T(8,128)S(1)} %get-tuple-element.22.speed_ref, f32[12,8,128]{2,1,0:T(8,128)S(1)} %collective-permute-done.7.rest_0_, f32[12,8,128]{2,1,0:T(8,128)S(1)} %collective-permute-done.8.rest_1_, ...), custom_call_target="tpu_custom_call" | custom-call | bytes 7000000 | tf_op jit(solution)/shard_map/moments/pallas_call | solution.py:674
  (14 shorter events, 0.1 us)
Async XLA Ops:
  2.1 12.8 %collective-permute-start.2 = (f32[49,8,128]{2,1,0:T(8,128)S(1)}, f32[49,8,128]{2,1,0:T(8,128)S(1)}, u32[]{:S(2)}, u32[]{:S(2)}) collective-permute-start(f32[49,8,128]{2,1,0:T(8,128)S(1)} %get-tuple-element.18.own_ref), channel_id=1, source_target_pairs={{0,1},{1,0},{2,4},{3,5},{4,2},{5,3},{6,8},{7,9},{8,6},{9,7},{10,12... | collective-permute-start | bytes 602120 | tf_op jit(solution)/shard_map/ppermute | solution.py:540
  10.2 5.9 %collective-permute-start.1 = (f32[49,8,128]{2,1,0:T(8,128)S(1)}, f32[49,8,128]{2,1,0:T(8,128)S(1)}, u32[]{:S(2)}, u32[]{:S(2)}) collective-permute-start(f32[49,8,128]{2,1,0:T(8,128)S(1)} %get-tuple-element.18.own_ref), channel_id=1, source_target_pairs={{0,2},{1,3},{2,0},{3,1},{4,6},{5,7},{6,4},{7,5},{8,10},{9,11},{10,... | collective-permute-start | bytes 602120 | tf_op jit(solution)/shard_map/ppermute | solution.py:541
  10.2 7.4 %collective-permute-start = (f32[49,8,128]{2,1,0:T(8,128)S(1)}, f32[49,8,128]{2,1,0:T(8,128)S(1)}, u32[]{:S(2)}, u32[]{:S(2)}) collective-permute-start(f32[49,8,128]{2,1,0:T(8,128)S(1)} %get-tuple-element.18.own_ref), channel_id=1, source_target_pairs={{0,1},{1,0},{2,3},{3,2},{4,5},{5,4},{6,7},{7,6},{8,9},{9,8},{10,11... | collective-permute-start | bytes 602120 | tf_op jit(solution)/shard_map/ppermute | solution.py:542
  14.9 2.7 %collective-permute-start.4 = (f32[49,8,128]{2,1,0:T(8,128)S(1)}, f32[49,8,128]{2,1,0:T(8,128)S(1)}, u32[]{:S(2)}, u32[]{:S(2)}) collective-permute-start(f32[49,8,128]{2,1,0:T(8,128)S(1)} %collective-permute-done.2.r3_ref), channel_id=1, source_target_pairs={{0,1},{1,0},{2,3},{3,2},{4,5},{5,4},{6,7},{7,6},{8,9},{9,8},{10,11... | collective-permute-start | bytes 602120 | tf_op jit(solution)/shard_map/ppermute | solution.py:547
  16.1 2.5 %collective-permute-start.3 = (f32[49,8,128]{2,1,0:T(8,128)S(1)}, f32[49,8,128]{2,1,0:T(8,128)S(1)}, u32[]{:S(2)}, u32[]{:S(2)}) collective-permute-start(f32[49,8,128]{2,1,0:T(8,128)S(1)} %collective-permute-done.1.r2_ref), channel_id=1, source_target_pairs={{0,1},{1,0},{2,3},{3,2},{4,5},{5,4},{6,7},{7,6},{8,9},{9,8},{10,11... | collective-permute-start | bytes 602120 | tf_op jit(solution)/shard_map/ppermute | solution.py:547
  31.3 9.7 %collective-permute-start.9 = (f32[12,8,128]{2,1,0:T(8,128)S(1)}, f32[12,8,128]{2,1,0:T(8,128)S(1)}, u32[]{:S(2)}, u32[]{:S(2)}) collective-permute-start(f32[12,8,128]{2,1,0:T(8,128)S(1)} %get-tuple-element.27.rest_0_), channel_id=1, source_target_pairs={{0,1},{1,0},{2,3},{3,2},{4,5},{5,4},{6,7},{7,6},{8,9},{9,8},{10,11... | collective-permute-start | bytes 147464 | tf_op jit(solution)/shard_map/ppermute | solution.py:542
  31.7 7.2 %collective-permute-start.6 = (f32[12,8,128]{2,1,0:T(8,128)S(1)}, f32[12,8,128]{2,1,0:T(8,128)S(1)}, u32[]{:S(2)}, u32[]{:S(2)}) collective-permute-start(f32[12,8,128]{2,1,0:T(8,128)S(1)} %get-tuple-element.27.rest_0_), channel_id=1, source_target_pairs={{0,1},{1,0},{2,4},{3,5},{4,2},{5,3},{6,8},{7,9},{8,6},{9,7},{10,12... | collective-permute-start | bytes 147464 | tf_op jit(solution)/shard_map/ppermute | solution.py:540
  36.3 3.2 %collective-permute-start.5 = (f32[12,8,128]{2,1,0:T(8,128)S(1)}, f32[12,8,128]{2,1,0:T(8,128)S(1)}, u32[]{:S(2)}, u32[]{:S(2)}) collective-permute-start(f32[12,8,128]{2,1,0:T(8,128)S(1)} %get-tuple-element.27.rest_0_), channel_id=1, source_target_pairs={{0,2},{1,3},{2,0},{3,1},{4,6},{5,7},{6,4},{7,5},{8,10},{9,11},{10,... | collective-permute-start | bytes 147464 | tf_op jit(solution)/shard_map/ppermute | solution.py:541
  39.5 2.4 %collective-permute-start.7 = (f32[12,8,128]{2,1,0:T(8,128)S(1)}, f32[12,8,128]{2,1,0:T(8,128)S(1)}, u32[]{:S(2)}, u32[]{:S(2)}) collective-permute-start(f32[12,8,128]{2,1,0:T(8,128)S(1)} %collective-permute-done.5.rest_2_), channel_id=1, source_target_pairs={{0,1},{1,0},{2,3},{3,2},{4,5},{5,4},{6,7},{7,6},{8,9},{9,8},{10,11... | collective-permute-start | bytes 147464 | tf_op jit(solution)/shard_map/ppermute | solution.py:547
  40.9 1.2 %collective-permute-start.8 = (f32[12,8,128]{2,1,0:T(8,128)S(1)}, f32[12,8,128]{2,1,0:T(8,128)S(1)}, u32[]{:S(2)}, u32[]{:S(2)}) collective-permute-start(f32[12,8,128]{2,1,0:T(8,128)S(1)} %collective-permute-done.6.rest_3_), channel_id=1, source_target_pairs={{0,1},{1,0},{2,3},{3,2},{4,5},{5,4},{6,7},{7,6},{8,9},{9,8},{10,11... | collective-permute-start | bytes 147464 | tf_op jit(solution)/shard_map/ppermute | solution.py:547
